TPU v7x, 32 devices: a whole 2x2x4 slice. The times are simulated.
32 devices in a mesh: view: 8 (over y, x, core), band: 4 (over z).
Axes of the slice: x: 2, y: 2, z: 4, core: 2. Of those that a mesh axis runs over, the one named last changes fastest.
Arguments:
- gaussians: float32 [512, 62, 256], P(('view', 'band')), may hold values from -8 to 128, as said below
- first_moment: float32 [512, 62, 256], P(('view', 'band')), may hold values from -0.6 to 0.6
- second_moment: float32 [512, 62, 256], P(('view', 'band')), may hold values from 0.0001 to 0.1
- camera: float32 [8, 9], P('view'), may hold values from -352 to 352, as said below
- target: float32 [8, 3, 64, 128], P('view', None, 'band'), may hold values from 0 to 1
- block_list: int32 [8, 4, 16], P('view', 'band'), may hold values from -1 to 511, as said below
- block_count: int32 [8, 4], P('view', 'band'), may hold values from 12 to 16, as said below
- tile_start: int32 [8, 4, 8], P('view', 'band'), may hold values from 0 to 15, as said below
- tile_end: int32 [8, 4, 8], P('view', 'band'), may hold values from 1 to 16, as said below
Outputs:
- new_gaussians: float32 [512, 62, 256], P(('view', 'band'))
- new_first_moment: float32 [512, 62, 256], P(('view', 'band'))
- new_second_moment: float32 [512, 62, 256], P(('view', 'band'))
- mean_loss: float32 [], replicated
- grads: float32 [512, 62, 256], P(('view', 'band'))
Inputs may be any that keep to these rules, and one draw needn't show every extreme that they name: Block k is held by device k // 16, devices counted with view slowest. Entry i of block_list[v, b] is a block for i < block_count[v, b] and -1 after; the live entries of one band are distinct, at most 1 of them are held by one device, and in every band some device holds exactly 1 of them. `block_count`: some band has exactly 16. tile_start < tile_end <= block_count of the band; tile_end - tile_start is at most 2, and exactly 2 for some tile of every band; the tiles of a band together cover every live position. `tile_end`: see tile_start. `gaussians`: component 9 of every Gaussian lies in [1, 2]; components 6 to 8 lie in [0, 2]. `camera`: A0 x A1 has a third entry of 0.6 or more.
All inputs are finite; a program needn't handle non-finite values.
Results may differ from a plain program's by a relative error of at most 0.0003.
Values sent between devices are 32-bit elements; how exact they have to be, the bound alone decides.
A program may use at most 128 MiB of HBM per device.

v0:
```python
import math

import jax
import jax.numpy as jnp
import numpy as np
from jax import lax
from jax.sharding import PartitionSpec as P

TILE = 16
ROWS = 16
COLS = 128
TILE_MOST = 2


HIGHEST_MODE = lax.Precision.HIGHEST
SSIM_WEIGHT = 0.2
ABS_WEIGHT = 0.8
STAB_MEAN = 0.0001
STAB_VAR = 0.0009
BIAS_FIRST = 1.0 - math.exp(100.0 * math.log(0.9))
BIAS_SECOND = 1.0 - math.exp(100.0 * math.log(0.999))
SH_ZERO = 0.28209479177387814
SH_ONE = 0.4886025119029199
SH_TWO = [
    1.0925484305920792,
    -1.0925484305920792,
    0.31539156525252005,
    -1.0925484305920792,
    0.5462742152960396,
]
SH_THREE = [
    -0.5900435899266435,
    2.890611442640554,
    -0.4570457994644658,
    0.3731763325901154,
    -0.4570457994644658,
    1.445305721320277,
    -0.5900435899266435,
]


def with_halo(array, sides, width):
    for axis, dim in sides:
        peers, length = (lax.axis_size(axis), array.shape[dim])
        up = [(i, (i + 1) % peers) for i in range(peers - 1)]
        down = [(j, i) for i, j in up]
        last = lax.slice_in_dim(array, length - width, length, axis=dim)
        leading = lax.slice_in_dim(array, 0, width, axis=dim)
        before = lax.ppermute(last, axis, up)
        after = lax.ppermute(leading, axis, down)
        array = jnp.concatenate([before, array, after], axis=dim)
    return array


def learning_rates():
    return np.concatenate(
        [
            np.full(6, 0.016),
            np.full(3, 0.005),
            np.full(4, 0.001),
            np.full(1, 0.05),
            np.full(3, 0.0025),
            np.full(45, 0.000125),
        ]
    ).astype(np.float32)


def kernel_taps():
    raw_taps = [math.exp(-(offset * offset) / 4.5) for offset in range(-5, 6)]
    tap_total = sum(raw_taps)
    return [raw_tap / tap_total for raw_tap in raw_taps]


def smooth(source, rows_out):
    kernel = kernel_taps()
    rows_done = kernel[0] * source[..., 0:rows_out, :]
    for offset in range(1, 11):
        rows_done = rows_done + kernel[offset] * source[..., offset : offset + rows_out, :]
    cols_n = source.shape[-1]
    padded = jnp.pad(rows_done, [(0, 0)] * (source.ndim - 1) + [(5, 5)])
    result = kernel[0] * padded[..., 0:cols_n]
    for offset in range(1, 11):
        result = result + kernel[offset] * padded[..., offset : offset + cols_n]
    return result


def ssim_value(mean_x, mean_y, square_x, square_y, cross_xy):
    var_x = square_x - mean_x * mean_x
    var_y = square_y - mean_y * mean_y
    covar = cross_xy - mean_x * mean_y
    upper = (2.0 * mean_x * mean_y + STAB_MEAN) * (2.0 * covar + STAB_VAR)
    lower = (mean_x * mean_x + mean_y * mean_y + STAB_MEAN) * (var_x + var_y + STAB_VAR)
    return upper / lower


def ssim_terms(pred_ext, target_ext, rows_out):
    mean_x = smooth(pred_ext, rows_out)
    mean_y = smooth(target_ext, rows_out)
    square_x = smooth(pred_ext * pred_ext, rows_out)
    square_y = smooth(target_ext * target_ext, rows_out)
    cross_xy = smooth(pred_ext * target_ext, rows_out)
    ssim_map, pullback = jax.vjp(ssim_value, mean_x, mean_y, square_x, square_y, cross_xy)
    partials = pullback(jnp.full_like(ssim_map, -SSIM_WEIGHT / 3.0))
    return (ssim_map, partials[0], partials[2], partials[4])


def harmonics(facing):
    dir_x, dir_y, dir_z = (facing[0], facing[1], facing[2])
    sq_x, sq_y, sq_z = (dir_x * dir_x, dir_y * dir_y, dir_z * dir_z)
    return jnp.stack(
        [
            SH_ZERO + 0.0 * dir_x,
            -SH_ONE * dir_y,
            SH_ONE * dir_z,
            -SH_ONE * dir_x,
            SH_TWO[0] * dir_x * dir_y,
            SH_TWO[1] * dir_y * dir_z,
            SH_TWO[2] * (2.0 * sq_z - sq_x - sq_y),
            SH_TWO[3] * dir_x * dir_z,
            SH_TWO[4] * (sq_x - sq_y),
            SH_THREE[0] * dir_y * (3.0 * sq_x - sq_y),
            SH_THREE[1] * dir_x * dir_y * dir_z,
            SH_THREE[2] * dir_y * (4.0 * sq_z - sq_x - sq_y),
            SH_THREE[3] * dir_z * (2.0 * sq_z - 3.0 * sq_x - 3.0 * sq_y),
            SH_THREE[4] * dir_x * (4.0 * sq_z - sq_x - sq_y),
            SH_THREE[5] * dir_z * (sq_x - sq_y),
            SH_THREE[6] * dir_x * (sq_x - 3.0 * sq_y),
        ]
    )


def project(window, cam_row):
    affine = cam_row[0:6].reshape(2, 3)
    cam_time = cam_row[8]
    centre = [window[:, axis_k, :] + cam_time * window[:, 3 + axis_k, :] for axis_k in range(3)]
    col_pos = (
        affine[0, 0] * centre[0] + affine[0, 1] * centre[1] + affine[0, 2] * centre[2] + cam_row[6]
    )
    row_pos = (
        affine[1, 0] * centre[0] + affine[1, 1] * centre[1] + affine[1, 2] * centre[2] + cam_row[7]
    )
    scales = [jnp.exp(window[:, 6 + axis_k, :]) for axis_k in range(3)]
    quat_len = jnp.sqrt(
        window[:, 9, :] * window[:, 9, :]
        + window[:, 10, :] * window[:, 10, :]
        + window[:, 11, :] * window[:, 11, :]
        + window[:, 12, :] * window[:, 12, :]
    )
    quat_r = window[:, 9, :] / quat_len
    quat_i = window[:, 10, :] / quat_len
    quat_j = window[:, 11, :] / quat_len
    quat_k = window[:, 12, :] / quat_len
    rotation = [
        [
            1.0 - 2.0 * (quat_j * quat_j + quat_k * quat_k),
            2.0 * (quat_i * quat_j - quat_r * quat_k),
            2.0 * (quat_i * quat_k + quat_r * quat_j),
        ],
        [
            2.0 * (quat_i * quat_j + quat_r * quat_k),
            1.0 - 2.0 * (quat_i * quat_i + quat_k * quat_k),
            2.0 * (quat_j * quat_k - quat_r * quat_i),
        ],
        [
            2.0 * (quat_i * quat_k - quat_r * quat_j),
            2.0 * (quat_j * quat_k + quat_r * quat_i),
            1.0 - 2.0 * (quat_i * quat_i + quat_j * quat_j),
        ],
    ]
    spread_rows = [
        [
            (
                affine[out_row, 0] * rotation[0][in_col]
                + affine[out_row, 1] * rotation[1][in_col]
                + affine[out_row, 2] * rotation[2][in_col]
            )
            * scales[in_col]
            for in_col in range(3)
        ]
        for out_row in range(2)
    ]
    conic_a = (
        spread_rows[0][0] * spread_rows[0][0]
        + spread_rows[0][1] * spread_rows[0][1]
        + spread_rows[0][2] * spread_rows[0][2]
        + 0.3
    )
    conic_b = (
        spread_rows[0][0] * spread_rows[1][0]
        + spread_rows[0][1] * spread_rows[1][1]
        + spread_rows[0][2] * spread_rows[1][2]
    )
    conic_c = (
        spread_rows[1][0] * spread_rows[1][0]
        + spread_rows[1][1] * spread_rows[1][1]
        + spread_rows[1][2] * spread_rows[1][2]
        + 0.3
    )
    determinant = conic_a * conic_c - conic_b * conic_b
    opacity = jax.nn.sigmoid(window[:, 13, :])
    normal = jnp.cross(affine[0], affine[1])
    facing = normal / jnp.sqrt(jnp.sum(normal * normal))
    sh_basis = harmonics(facing)
    sh_coef = window[:, 14:, :].reshape(window.shape[0], 16, 3, window.shape[2])
    colour = 0.5 + jnp.einsum("k,tkcb->ctb", sh_basis, sh_coef, precision=HIGHEST_MODE)
    return (col_pos, row_pos, conic_a, conic_b, conic_c, determinant, opacity, colour)


def record_stack(window, cam_row):
    col_pos, row_pos, conic_a, conic_b, conic_c, determinant, opacity, colour = project(
        window, cam_row
    )
    return jnp.stack(
        [col_pos, row_pos, conic_a, conic_b, conic_c, opacity, colour[0], colour[1], colour[2]],
        axis=1,
    )


def blend_tile(records, first_pos, live_low, live_high, row_start, col_start):
    window_len = records.shape[0]
    block_len = records.shape[2]
    col_pos = records[:, 0, :]
    row_pos = records[:, 1, :]
    conic_a = records[:, 2, :]
    conic_b = records[:, 3, :]
    conic_c = records[:, 4, :]
    opacity = records[:, 5, :]
    colour = jnp.stack([records[:, 6, :], records[:, 7, :], records[:, 8, :]])
    determinant = conic_a * conic_c - conic_b * conic_b
    positions = first_pos + jnp.arange(window_len, dtype=jnp.int32)
    is_live = (positions >= live_low) & (positions < live_high)
    live_flat = jnp.repeat(is_live, block_len)
    pixels = jnp.arange(TILE * TILE, dtype=jnp.int32)
    pix_row = (row_start + pixels // TILE).astype(jnp.float32) + 0.5
    pix_col = (col_start + pixels % TILE).astype(jnp.float32) + 0.5
    delta_col = pix_col[None, :] - col_pos.reshape(-1)[:, None]
    delta_row = pix_row[None, :] - row_pos.reshape(-1)[:, None]
    exponent = (
        -0.5
        * (
            conic_c.reshape(-1)[:, None] * delta_col * delta_col
            - 2.0 * conic_b.reshape(-1)[:, None] * delta_col * delta_row
            + conic_a.reshape(-1)[:, None] * delta_row * delta_row
        )
        / determinant.reshape(-1)[:, None]
    )
    alphas = jnp.where(live_flat[:, None], opacity.reshape(-1)[:, None] * jnp.exp(exponent), 0.0)
    keep_log = jnp.log1p(-alphas).reshape(window_len, block_len, -1)
    inner_sum = jnp.cumsum(keep_log, axis=1)
    block_total = inner_sum[:, -1, :]
    outer_sum = jnp.cumsum(block_total, axis=0) - block_total
    log_trans = inner_sum - keep_log + outer_sum[:, None, :]
    weight = alphas * jnp.exp(log_trans.reshape(window_len * block_len, -1))
    return jnp.dot(colour.reshape(3, -1), weight, precision=HIGHEST_MODE)


def tile_frame(tile_index, starts, list_len, row_base):
    tile_cols = COLS // TILE
    first_pos = jnp.minimum(starts[tile_index], list_len - TILE_MOST).astype(jnp.int32)
    row_start = row_base + tile_index // tile_cols * TILE
    col_start = tile_index % tile_cols * TILE
    return (first_pos, row_start, col_start)


def from_tiles(tiles_out):
    tile_rows = ROWS // TILE
    tile_cols = COLS // TILE
    return (
        tiles_out.reshape(tile_rows, tile_cols, 3, TILE, TILE)
        .transpose(2, 0, 3, 1, 4)
        .reshape(3, ROWS, COLS)
    )


def to_tiles(image):
    tile_rows = ROWS // TILE
    tile_cols = COLS // TILE
    return (
        image.reshape(3, tile_rows, TILE, tile_cols, TILE)
        .transpose(1, 3, 0, 2, 4)
        .reshape(tile_rows * tile_cols, 3, TILE * TILE)
    )


def render_band(listed, tile_render, starts, endings, row_base):
    list_len = listed.shape[0]

    def draw_tile(tile_index):
        first_pos, row_start, col_start = tile_frame(tile_index, starts, list_len, row_base)
        window = lax.dynamic_slice_in_dim(listed, first_pos, TILE_MOST, 0)
        return tile_render(
            window, first_pos, starts[tile_index], endings[tile_index], row_start, col_start
        )

    tiles_out = lax.map(draw_tile, jnp.arange(starts.shape[0], dtype=jnp.int32))
    return from_tiles(tiles_out)


def backward_band(listed, tile_render, starts, endings, row_base, grad_pred):
    list_len = listed.shape[0]
    cot_tiles = to_tiles(grad_pred)

    def tile_back(summed, tile_index):
        first_pos, row_start, col_start = tile_frame(tile_index, starts, list_len, row_base)
        window = lax.dynamic_slice_in_dim(listed, first_pos, TILE_MOST, 0)

        def draw_window(chosen):
            return tile_render(
                chosen, first_pos, starts[tile_index], endings[tile_index], row_start, col_start
            )

        unused, pullback = jax.vjp(draw_window, window)
        grad_window = pullback(cot_tiles[tile_index])[0]
        current = lax.dynamic_slice_in_dim(summed, first_pos, TILE_MOST, 0)
        summed = lax.dynamic_update_slice_in_dim(summed, current + grad_window, first_pos, 0)
        return (summed, None)

    summed, unused = lax.scan(
        tile_back, jnp.zeros_like(listed), jnp.arange(starts.shape[0], dtype=jnp.int32)
    )
    return summed


def adam_update(params, moment_one, moment_two, gradient):
    learn_rates = jnp.asarray(learning_rates())[None, :, None]
    new_one = 0.9 * moment_one + 0.1 * gradient
    new_two = 0.999 * moment_two + 0.001 * gradient * gradient
    change = learn_rates * (new_one / BIAS_FIRST) / (jnp.sqrt(new_two / BIAS_SECOND) + 1e-08)
    return (params - change, new_one, new_two)


def per_device(
    gaussians,
    first_moment,
    second_moment,
    camera,
    target,
    block_list,
    block_count,
    tile_start,
    tile_end,
):
    views_n = lax.axis_size("view")
    bands_n = lax.axis_size("band")
    devices = views_n * bands_n
    blk_local = gaussians.shape[0]
    comp_count = gaussians.shape[1]
    block_len = gaussians.shape[2]
    list_len = block_list.shape[2]
    per_owner = max(1, 4 * list_len // (3 * devices))
    slot_total = devices * per_owner
    block_ids = block_list[0, 0]
    live_count = block_count[0, 0]
    position = jnp.arange(list_len, dtype=jnp.int32)
    is_live = position < live_count
    owners = jnp.where(is_live, block_ids // blk_local, -1)
    local_ids = jnp.where(is_live, block_ids % blk_local, -1)
    earlier = (
        (owners[:, None] == owners[None, :])
        & (position[None, :] < position[:, None])
        & is_live[None, :]
    )
    slot_rank = jnp.sum(earlier.astype(jnp.int32), axis=1)
    slot_of = jnp.where(is_live, owners * per_owner + slot_rank, slot_total)
    slot_hit = slot_of[:, None] == jnp.arange(slot_total, dtype=jnp.int32)[None, :]
    request = jnp.max(jnp.where(slot_hit, local_ids[:, None], -1), axis=0)
    wanted = lax.all_to_all(
        request.reshape(devices, per_owner),
        ("view", "band"),
        split_axis=0,
        concat_axis=0,
        tiled=True,
    ).reshape(slot_total)
    picker = (wanted[:, None] == jnp.arange(blk_local, dtype=jnp.int32)[None, :]).astype(
        jnp.float32
    )
    payload = jnp.dot(picker, gaussians.reshape(blk_local, -1), precision=HIGHEST_MODE).reshape(
        slot_total, comp_count, block_len
    )
    param_filler = jnp.broadcast_to(
        (jnp.arange(comp_count) == 9).astype(jnp.float32)[:, None], (comp_count, block_len)
    )
    record_index = jnp.arange(9)
    record_filler = jnp.broadcast_to(
        ((record_index == 2) | (record_index == 4)).astype(jnp.float32)[:, None], (9, block_len)
    )
    all_cameras = lax.all_gather(camera, "view", axis=0, tiled=True)
    slot_view = jnp.arange(slot_total, dtype=jnp.int32) // (per_owner * bands_n)
    view_pick = (slot_view[:, None] == jnp.arange(views_n, dtype=jnp.int32)[None, :]).astype(
        jnp.float32
    )
    slot_cameras = jnp.dot(view_pick, all_cameras, precision=HIGHEST_MODE)
    safe_payload = jnp.where((wanted >= 0)[:, None, None], payload, param_filler[None])

    def owner_records(blocks):

        def one_record(one_block, one_camera):
            return record_stack(one_block[None], one_camera)[0]

        return jax.vmap(one_record)(blocks, slot_cameras)

    records_sent, owner_pullback = jax.vjp(owner_records, safe_payload)
    received = lax.all_to_all(
        records_sent, ("view", "band"), split_axis=0, concat_axis=0, tiled=True
    )

    def tile_render(window, first_pos, live_low, live_high, row_start, col_start):
        return blend_tile(window, first_pos, live_low, live_high, row_start, col_start)

    listed = jnp.take(received, jnp.minimum(slot_of, slot_total - 1), axis=0)
    listed = jnp.where(is_live[:, None, None], listed, record_filler[None])
    band_index = lax.axis_index("band")
    row_base = band_index * ROWS
    starts = tile_start[0, 0]
    endings = tile_end[0, 0]
    predicted = render_band(listed, tile_render, starts, endings, row_base)
    target_band = target[0]
    stacked = jnp.stack([predicted, target_band])
    padded = with_halo(stacked, (("band", 2),), 5)
    ssim_map, part_mean, part_square, part_cross = ssim_terms(padded[0], padded[1], ROWS)
    adjoint = with_halo(jnp.stack([part_mean, part_square, part_cross]), (("band", 2),), 5)
    spread = smooth(adjoint, ROWS)
    error_map = predicted - target_band
    grad_pred = (
        ABS_WEIGHT / 3.0 * jnp.sign(error_map)
        + spread[0]
        + 2.0 * predicted * spread[1]
        + target_band * spread[2]
    )
    local_loss = jnp.sum(
        ABS_WEIGHT / 3.0 * jnp.abs(error_map) + SSIM_WEIGHT / 3.0 * (1.0 - ssim_map)
    )
    loss_sum = lax.psum(local_loss, ("view", "band"))
    mean_loss = loss_sum / (devices * ROWS * COLS)
    grads_list = backward_band(listed, tile_render, starts, endings, row_base, grad_pred)
    record_width = grads_list.shape[1]
    outgoing = jnp.dot(
        slot_hit.astype(jnp.float32).T, grads_list.reshape(list_len, -1), precision=HIGHEST_MODE
    ).reshape(slot_total, record_width, block_len)
    incoming = lax.all_to_all(outgoing, ("view", "band"), split_axis=0, concat_axis=0, tiled=True)
    grad_payload = owner_pullback(incoming)[0]
    gradient = jnp.dot(
        picker.T, grad_payload.reshape(slot_total, -1), precision=HIGHEST_MODE
    ).reshape(blk_local, comp_count, block_len)
    new_params, new_one, new_two = adam_update(gaussians, first_moment, second_moment, gradient)
    return (new_params, new_one, new_two, mean_loss, gradient)


def solution(mesh):
    return jax.shard_map(
        per_device,
        mesh=mesh,
        in_specs=(
            P(("view", "band"), None, None),
            P(("view", "band"), None, None),
            P(("view", "band"), None, None),
            P("view", None),
            P("view", None, "band", None),
            P("view", "band", None),
            P("view", "band"),
            P("view", "band", None),
            P("view", "band", None),
        ),
        out_specs=(
            P(("view", "band"), None, None),
            P(("view", "band"), None, None),
            P(("view", "band"), None, None),
            P(),
            P(("view", "band"), None, None),
        ),
        check_vma=False,
    )
```

profile of v0, /device:TPU:0, one launch (start us, length us, event | category | flops | bytes accessed | tf_op | source)
XLA Modules:
  0.0 407.5 jit_solution(10353391427043468313)
XLA Ops:
  2.9 7.3 %all-to-all-start = ((s32[32,1,1]{2,1,0:T(1,128)}), s32[32,1,1]{2,1,0:T(1,128)S(1)}, u32[]{:S(2)}, u32[]{:S(2)}) async-start(s32[32,1,1]{2,1,0:T(1,128)} %copy.200), calls=%async_computation | async-start | bytes 32768 | tf_op jit(solution)/shard_map/all_to_all | solution.py:367
  10.3 9.1 %all-gather = f32[8,1,9]{2,1,0:T(1,128)S(1)} all-gather(f32[1,1,9]{2,1,0:T(1,128)} %bitcast.719), channel_id=1, replica_groups=mesh['view'=8,'band'=4] {'view'}, dimensions={0}, use_global_device_ids=true | all-gather | bytes 324 | tf_op jit(solution)/shard_map/all_gather | solution.py:387
  21.3 2.2 select_bitcast_fusion
  27.8 4.5 %all-to-all-start.1 = ((f32[32,9,256]{2,1,0:T(8,128)}), f32[32,9,256]{2,1,0:T(8,128)S(1)}, u32[]{:S(2)}, u32[]{:S(2)}) async-start(f32[32,9,256]{2,1,0:T(8,128)} %copy.203), calls=%async_computation.1 | async-start | bytes 1048576 | tf_op jit(solution)/shard_map/all_to_all | solution.py:403
  32.5 14.2 %all-to-all-done.1 = f32[32,9,256]{2,1,0:T(8,128)S(1)} async-done(((f32[32,9,256]{2,1,0:T(8,128)}), f32[32,9,256]{2,1,0:T(8,128)S(1)}, u32[]{:S(2)}, u32[]{:S(2)}) %all-to-all-start.1) | async-done | bytes 294944 | tf_op jit(solution)/shard_map/all_to_all | solution.py:403
  47.5 107.2 %while.26 = (s32[]{:T(128)}, f32[8,3,256]{2,0,1:T(8,128)S(1)}, s32[8]{0:T(128)S(1)}, s32[8]{0:T(128)S(1)}, f32[16,9,256]{2,0,1:T(8,128)S(1)}, /*index=5*/s32[8]{...) while((s32[]{:T(128)}, f32[8,3,256]{2,0,1:T(8,128)S(1)}, ...), condition=%wide.region_7.8_spmd, body=%wide.region_3.7_spmd.sunk | while | flops 27670572 | bytes 5517015 | solution.py:295
  56.5 2.1 fusion.481
  83.3 2.1 fusion.481
  96.7 2.1 fusion.481
  155.0 4.5 %collective-permute-start = (f32[2,3,5,128]{3,2,1,0:T(8,128)S(1)}, f32[2,3,5,128]{3,2,1,0:T(8,128)S(1)}, u32[]{:S(2)}, u32[]{:S(2)}) collective-permute-start(f32[2,3,5,128]{3,2,1,0:T(8,128)S(1)} %get-tuple-element.533), channel_id=1, source_target_pairs={{0,1},{1,2},{2,3},{4,5},{5,6},{6,7},{8,9},{9,10},{10,11},{12,13},{... | collective-permute-start | bytes 46088 | tf_op jit(solution)/shard_map/ppermute | solution.py:49
  161.0 4.2 %collective-permute-done.1 = f32[2,3,5,128]{3,2,1,0:T(8,128)S(1)} collective-permute-done((f32[2,3,5,128]{3,2,1,0:T(8,128)S(1)}, f32[2,3,5,128]{3,2,1,0:T(8,128)S(1)}, u32[]{:S(2)}, u32[]{:S(2)}) %collective-permute-start.1) | collective-permute-done | bytes 15392 | tf_op jit(solution)/shard_map/ppermute | solution.py:50
  170.1 4.2 %collective-permute-done.3 = f32[3,3,5,128]{3,2,1,0:T(8,128)S(1)} collective-permute-done((f32[3,3,5,128]{3,2,1,0:T(8,128)S(1)}, f32[3,3,5,128]{3,2,1,0:T(8,128)S(1)}, u32[]{:S(2)}, u32[]{:S(2)}) %collective-permute-start.3) | collective-permute-done | bytes 23072 | tf_op jit(solution)/shard_map/ppermute | solution.py:50
  175.4 174.2 %while.27 = (s32[]{:T(128)}, f32[16,9,256]{2,0,1:T(8,128)S(1)}, s32[8]{0:T(128)S(1)}, s32[8]{0:T(128)S(1)}, f32[8,3,256]{2,0,1:T(8,128)S(1)}, /*index=5*/s32[8]{...) while((s32[]{:T(128)}, f32[16,9,256]{2,0,1:T(8,128)S(1)}, ...), condition=%wide.region_23.24_spmd, body=%wide.region_8.23_spmd.sunk | while | flops 58650668 | bytes 16278771 | solution.py:318
  189.6 4.6 %fusion.493 = f32[2,256,2,128]{1,2,3,0:T(2,128)S(1)} fusion(f32[2,256,2,128]{1,3,2,0:T(8,128)S(1)} %bitcast.643), kind=kOutput, calls=%fused_computation.171.clone.1 | output fusion | flops 16646144 | bytes 1048576 | tf_op jit(solution)/shard_map/reduce-window.28
  211.3 4.6 %fusion.493 = f32[2,256,2,128]{1,2,3,0:T(2,128)S(1)} fusion(f32[2,256,2,128]{1,3,2,0:T(8,128)S(1)} %bitcast.643), kind=kOutput, calls=%fused_computation.171.clone.1 | output fusion | flops 16646144 | bytes 1048576 | tf_op jit(solution)/shard_map/reduce-window.28
  233.1 4.6 %fusion.493 = f32[2,256,2,128]{1,2,3,0:T(2,128)S(1)} fusion(f32[2,256,2,128]{1,3,2,0:T(8,128)S(1)} %bitcast.643), kind=kOutput, calls=%fused_computation.171.clone.1 | output fusion | flops 16646144 | bytes 1048576 | tf_op jit(solution)/shard_map/reduce-window.28
  254.9 4.6 %fusion.493 = f32[2,256,2,128]{1,2,3,0:T(2,128)S(1)} fusion(f32[2,256,2,128]{1,3,2,0:T(8,128)S(1)} %bitcast.643), kind=kOutput, calls=%fused_computation.171.clone.1 | output fusion | flops 16646144 | bytes 1048576 | tf_op jit(solution)/shard_map/reduce-window.28
  276.6 4.6 %fusion.493 = f32[2,256,2,128]{1,2,3,0:T(2,128)S(1)} fusion(f32[2,256,2,128]{1,3,2,0:T(8,128)S(1)} %bitcast.643), kind=kOutput, calls=%fused_computation.171.clone.1 | output fusion | flops 16646144 | bytes 1048576 | tf_op jit(solution)/shard_map/reduce-window.28
  298.4 4.6 %fusion.493 = f32[2,256,2,128]{1,2,3,0:T(2,128)S(1)} fusion(f32[2,256,2,128]{1,3,2,0:T(8,128)S(1)} %bitcast.643), kind=kOutput, calls=%fused_computation.171.clone.1 | output fusion | flops 16646144 | bytes 1048576 | tf_op jit(solution)/shard_map/reduce-window.28
  320.1 4.6 %fusion.493 = f32[2,256,2,128]{1,2,3,0:T(2,128)S(1)} fusion(f32[2,256,2,128]{1,3,2,0:T(8,128)S(1)} %bitcast.643), kind=kOutput, calls=%fused_computation.171.clone.1 | output fusion | flops 16646144 | bytes 1048576 | tf_op jit(solution)/shard_map/reduce-window.28
  341.9 4.6 %fusion.493 = f32[2,256,2,128]{1,2,3,0:T(2,128)S(1)} fusion(f32[2,256,2,128]{1,3,2,0:T(8,128)S(1)} %bitcast.643), kind=kOutput, calls=%fused_computation.171.clone.1 | output fusion | flops 16646144 | bytes 1048576 | tf_op jit(solution)/shard_map/reduce-window.28
  351.0 2.7 all-to-all-start.2
  353.8 41.0 %psum.7 = f32[]{:T(128)} all-reduce(f32[]{:T(128)} %get-tuple-element.415), channel_id=1, replica_groups=mesh['view'=8,'band'=4] {'view','band'}, use_global_device_ids=true, to_apply=%region_25.26 | all-reduce | flops 1 | bytes 8 | tf_op jit(solution)/shard_map/psum | solution.py:433
  399.9 6.5 %divide_subtract_fusion = (f32[16,62,256]{2,0,1:T(8,128)}, f32[16,62,256]{2,0,1:T(8,128)}, f32[16,62,256]{2,0,1:T(8,128)}, f32[16,62,256]{2,0,1:T(8,128)}) fusion(f32[16,62,256]{2,0,1:T(8,128)S(1)} %copy-done.1, f32[62]{0:T(128)S(1)} %copy-done.8, f32[16,62,256]{2,0,1:T(8,128)S(1)} %copy-done.4, f32[16,62,256]{2,0,1:T(8,128)S(1)} %copy-done.5, ...), kind=kOutput, calls=%fused_computation.272 | convolution fusion | flops 111739392 | bytes 9273720 | tf_op jit(solution)/shard_map/dot_general | solution.py:442
  (1096 shorter events, 182.0 us)
Async XLA Ops:
  2.9 17.0 %all-to-all-start = ((s32[32,1,1]{2,1,0:T(1,128)}), s32[32,1,1]{2,1,0:T(1,128)S(1)}, u32[]{:S(2)}, u32[]{:S(2)}) async-start(s32[32,1,1]{2,1,0:T(1,128)} %copy.200), calls=%async_computation | async-start | bytes 32768 | tf_op jit(solution)/shard_map/all_to_all | solution.py:367
  23.5 1.3 copy-start
  24.9 7.6 %copy-start.3 = (s32[1,1,16]{2,1,0:T(1,128)S(1)}, s32[1,1,16]{2,1,0:T(1,128)}, u32[]{:S(2)}) copy-start(s32[1,1,16]{2,1,0:T(1,128)} %param.19) | copy-start | bytes 196
  26.8 20.7 %copy-start.6 = (s32[1,1,8]{2,1,0:T(1,128)S(1)}, s32[1,1,8]{2,1,0:T(1,128)}, u32[]{:S(2)}) copy-start(s32[1,1,8]{2,1,0:T(1,128)} %param.21) | copy-start | bytes 100
  26.8 20.7 %copy-start.7 = (s32[1,1,8]{2,1,0:T(1,128)S(1)}, s32[1,1,8]{2,1,0:T(1,128)}, u32[]{:S(2)}) copy-start(s32[1,1,8]{2,1,0:T(1,128)} %param.22) | copy-start | bytes 100
  27.8 18.8 %all-to-all-start.1 = ((f32[32,9,256]{2,1,0:T(8,128)}), f32[32,9,256]{2,1,0:T(8,128)S(1)}, u32[]{:S(2)}, u32[]{:S(2)}) async-start(f32[32,9,256]{2,1,0:T(8,128)} %copy.203), calls=%async_computation.1 | async-start | bytes 1048576 | tf_op jit(solution)/shard_map/all_to_all | solution.py:403
  47.5 107.5 %copy-start.2 = (f32[1,3,16,128]{3,2,1,0:T(8,128)S(1)}, f32[1,3,16,128]{3,2,1,0:T(8,128)}, u32[]{:S(2)}) copy-start(f32[1,3,16,128]{3,2,1,0:T(8,128)} %param.18) | copy-start | bytes 73732
  155.0 6.0 %collective-permute-start = (f32[2,3,5,128]{3,2,1,0:T(8,128)S(1)}, f32[2,3,5,128]{3,2,1,0:T(8,128)S(1)}, u32[]{:S(2)}, u32[]{:S(2)}) collective-permute-start(f32[2,3,5,128]{3,2,1,0:T(8,128)S(1)} %get-tuple-element.533), channel_id=1, source_target_pairs={{0,1},{1,2},{2,3},{4,5},{5,6},{6,7},{8,9},{9,10},{10,11},{12,13},{... | collective-permute-start | bytes 46088 | tf_op jit(solution)/shard_map/ppermute | solution.py:49
  159.5 5.7 %collective-permute-start.1 = (f32[2,3,5,128]{3,2,1,0:T(8,128)S(1)}, f32[2,3,5,128]{3,2,1,0:T(8,128)S(1)}, u32[]{:S(2)}, u32[]{:S(2)}) collective-permute-start(f32[2,3,5,128]{3,2,1,0:T(8,128)S(1)} %get-tuple-element.534), channel_id=1, source_target_pairs={{1,0},{2,1},{3,2},{5,4},{6,5},{7,6},{9,8},{10,9},{11,10},{13,12},{... | collective-permute-start | bytes 46088 | tf_op jit(solution)/shard_map/ppermute | solution.py:50
  166.6 3.5 collective-permute-start.2
  168.5 5.9 %collective-permute-start.3 = (f32[3,3,5,128]{3,2,1,0:T(8,128)S(1)}, f32[3,3,5,128]{3,2,1,0:T(8,128)S(1)}, u32[]{:S(2)}, u32[]{:S(2)}) collective-permute-start(f32[3,3,5,128]{3,2,1,0:T(8,128)S(1)} %get-tuple-element.531), channel_id=1, source_target_pairs={{1,0},{2,1},{3,2},{5,4},{6,5},{7,6},{9,8},{10,9},{11,10},{13,12},{... | collective-permute-start | bytes 69128 | tf_op jit(solution)/shard_map/ppermute | solution.py:50
  351.0 44.4 %all-to-all-start.2 = ((f32[32,9,256]{2,1,0:T(8,128)}), f32[32,9,256]{2,1,0:T(8,128)S(1)}, u32[]{:S(2)}, u32[]{:S(2)}) async-start(f32[32,9,256]{2,1,0:T(8,128)} %copy.216), calls=%async_computation.2 | async-start | bytes 1048576 | tf_op jit(solution)/shard_map/all_to_all | solution.py:440
  396.8 3.1 copy-start.1
  396.8 3.1 copy-start.4
  396.8 3.1 copy-start.5
  396.8 3.1 copy-start.8
where the time goes:
time: 410 us; the launch traced here: 408 us
  other arithmetic  145 us (35%)
  loops' own time  78 us (19%)
  local copies, waits for them, and re-layouts  58 us (14%)
  blocking collectives  50.1 us (12%)
  matrix products  26.2 us (6%)
  starting transfers between devices  23.6 us (6%)
  waiting for transfers between devices  22.9 us (6%)
    another operation x73, other arithmetic  76.2 us
    psum x1, blocking collectives, per_device(): loss_sum = lax.psum(local_loss, ('view', 'band'))  41 us
    another operation x1, loops' own time, backward_band(): lax.scan(tile_back, jnp.zeros_like(listed), jnp.arange(starts.shape[0], d...  39.4 us
    another operation x1, loops' own time, render_band(): tiles_out = lax.map(draw_tile, jnp.arange(starts.shape[0], dtype=jnp.int32))  38.6 us
    and x16, other arithmetic, blend_tile(): is_live = (positions >= live_low) & (positions < live_high)  20.8 us
    dot_general x24, matrix products, blend_tile(): return jnp.dot(colour.reshape(3, -1), weight, precision=HIGHEST_MODE)  14.9 us
    all_to_all x1, waiting for transfers between devices, per_device(): lax.all_to_all(records_sent, ('view', 'band'), split_axis=0, concat_axis=...  14.2 us
    mul x16, other arithmetic, blend_tile(): weight = alphas * jnp.exp(log_trans.reshape(window_len * block_len, -1))  12 us
  transfers between devices with their start and end apart: 7, of which 5 were waited for; matrix products, arithmetic and copies ran while one was open for 0% of the time, Pallas kernels for 0%

commit v1 on v0

v1 whole, which is shorter than its diff:
```python
import functools
import math

import jax
import jax.numpy as jnp
import numpy as np
from jax import lax
from jax.experimental import pallas as pl
from jax.experimental.pallas import tpu as pltpu
from jax.sharding import PartitionSpec as P

TILE = 16
TILE_MOST = 2
HALO = 5
REACH = 2 * HALO
ROW_REC = 9

HIGHEST_MODE = lax.Precision.HIGHEST
SSIM_WEIGHT = 0.2
ABS_WEIGHT = 0.8
STAB_MEAN = 0.0001
STAB_VAR = 0.0009
BIAS_FIRST = 1.0 - math.exp(100.0 * math.log(0.9))
BIAS_SECOND = 1.0 - math.exp(100.0 * math.log(0.999))
LOG2_E = math.log2(math.e)
SH_ZERO = 0.28209479177387814
SH_ONE = 0.4886025119029199
SH_TWO = [
    1.0925484305920792,
    -1.0925484305920792,
    0.31539156525252005,
    -1.0925484305920792,
    0.5462742152960396,
]
SH_THREE = [
    -0.5900435899266435,
    2.890611442640554,
    -0.4570457994644658,
    0.3731763325901154,
    -0.4570457994644658,
    1.445305721320277,
    -0.5900435899266435,
]
F32 = jnp.float32
BF16 = jnp.bfloat16
MESH = pl.DeviceIdType.MESH
NEVER = -1e30


def learning_rates():
    return np.concatenate(
        [
            np.full(6, 0.016),
            np.full(3, 0.005),
            np.full(4, 0.001),
            np.full(1, 0.05),
            np.full(3, 0.0025),
            np.full(45, 0.000125),
        ]
    ).astype(np.float32)


def kernel_taps():
    raw_taps = [math.exp(-(offset * offset) / 4.5) for offset in range(-5, 6)]
    tap_total = sum(raw_taps)
    return [raw_tap / tap_total for raw_tap in raw_taps]


def up8(value):
    return (value + 7) // 8 * 8


def smoothing_tables(rows, cols, channels):
    taps = kernel_taps()
    in_rows, mid_rows = up8(rows + 2 * REACH), up8(rows + REACH)
    across = np.zeros((cols, cols), np.float32)
    for out in range(cols):
        for m in range(-HALO, HALO + 1):
            if 0 <= out + m < cols:
                across[out + m, out] = taps[m + HALO]
    first = np.zeros((channels * mid_rows, channels * in_rows), np.float32)
    second = np.zeros((channels * rows, channels * mid_rows), np.float32)
    for c in range(channels):
        for e in range(rows + REACH):
            for m in range(REACH + 1):
                first[c * mid_rows + e, c * in_rows + e + m] = taps[m]
        for i in range(rows):
            for m in range(REACH + 1):
                second[c * rows + i, c * mid_rows + i + m] = taps[m]
    return across, first, second


def power_table(tiles, cols):
    lane = np.arange(cols)
    local = lane % TILE + 0.5 - TILE / 2
    belongs = (lane[None, :] // TILE == np.arange(tiles)[:, None]).astype(np.float32)
    return np.concatenate([belongs, belongs * local, belongs * local * local]).astype(np.float32)


def harmonics(dir_x, dir_y, dir_z):
    sq_x, sq_y, sq_z = (dir_x * dir_x, dir_y * dir_y, dir_z * dir_z)
    return [
        SH_ZERO + 0.0 * dir_x,
        -SH_ONE * dir_y,
        SH_ONE * dir_z,
        -SH_ONE * dir_x,
        SH_TWO[0] * dir_x * dir_y,
        SH_TWO[1] * dir_y * dir_z,
        SH_TWO[2] * (2.0 * sq_z - sq_x - sq_y),
        SH_TWO[3] * dir_x * dir_z,
        SH_TWO[4] * (sq_x - sq_y),
        SH_THREE[0] * dir_y * (3.0 * sq_x - sq_y),
        SH_THREE[1] * dir_x * dir_y * dir_z,
        SH_THREE[2] * dir_y * (4.0 * sq_z - sq_x - sq_y),
        SH_THREE[3] * dir_z * (2.0 * sq_z - 3.0 * sq_x - 3.0 * sq_y),
        SH_THREE[4] * dir_x * (4.0 * sq_z - sq_x - sq_y),
        SH_THREE[5] * dir_z * (sq_x - sq_y),
        SH_THREE[6] * dir_x * (sq_x - 3.0 * sq_y),
    ]


def camera_basis(affine):
    a, b = affine[0:3], affine[3:6]
    n_x = a[1] * b[2] - a[2] * b[1]
    n_y = a[2] * b[0] - a[0] * b[2]
    n_z = a[0] * b[1] - a[1] * b[0]
    length = jnp.sqrt(n_x * n_x + n_y * n_y + n_z * n_z)
    return harmonics(n_x / length, n_y / length, n_z / length)


def shape_of(affine, logs, quats, logit):
    scales = [jnp.exp(value) for value in logs]
    quat_len = jnp.sqrt(
        quats[0] * quats[0] + quats[1] * quats[1] + quats[2] * quats[2] + quats[3] * quats[3]
    )
    r, i, j, k = [value / quat_len for value in quats]
    rotation = [
        [1.0 - 2.0 * (j * j + k * k), 2.0 * (i * j - r * k), 2.0 * (i * k + r * j)],
        [2.0 * (i * j + r * k), 1.0 - 2.0 * (i * i + k * k), 2.0 * (j * k - r * i)],
        [2.0 * (i * k - r * j), 2.0 * (j * k + r * i), 1.0 - 2.0 * (i * i + j * j)],
    ]
    m = [
        [
            (
                affine[3 * o] * rotation[0][c]
                + affine[3 * o + 1] * rotation[1][c]
                + affine[3 * o + 2] * rotation[2][c]
            )
            * scales[c]
            for c in range(3)
        ]
        for o in range(2)
    ]
    conic_a = m[0][0] * m[0][0] + m[0][1] * m[0][1] + m[0][2] * m[0][2] + 0.3
    conic_b = m[0][0] * m[1][0] + m[0][1] * m[1][1] + m[0][2] * m[1][2]
    conic_c = m[1][0] * m[1][0] + m[1][1] * m[1][1] + m[1][2] * m[1][2] + 0.3
    opacity = 1.0 / (1.0 + jnp.exp(-logit))
    return conic_a, conic_b, conic_c, opacity


def split3(value, axis=0):
    high = value.astype(BF16)
    rest = value - high.astype(F32)
    middle = rest.astype(BF16)
    low = (rest - middle.astype(F32)).astype(BF16)
    return high, middle, low


def exact_dot(table, value, dims):
    table = table.astype(BF16)
    total = None
    for part in split3(value):
        term = lax.dot_general(table, part, (dims, ((), ())), preferred_element_type=F32)
        total = term if total is None else total + term
    return total


def expand_dot(value, table):
    table = table.astype(BF16)
    total = None
    for part in split3(value):
        term = lax.dot_general(
            part, table, (((0,), (0,)), ((), ())), preferred_element_type=F32
        )
        total = term if total is None else total + term
    return total


NN = ((1,), (0,))
NT = ((1,), (1,))


def requests_of(messages, base, list_len, blocks):
    devices = messages.shape[0]
    block_iota = lax.broadcasted_iota(jnp.int32, (devices, blocks), 1).astype(F32) + base
    hit = jnp.zeros((devices, blocks), F32)
    for i in range(list_len):
        wanted = messages[:, 16 + i : 17 + i]
        hit = hit + jnp.where(wanted == block_iota, 1.0, 0.0)
    return hit


def tree_sum(vregs, lane_count):
    sub = lax.broadcasted_iota(jnp.int32, (8, lane_count), 0)

    def join(a, b, mask, shift):
        return jnp.where(mask, a, b) + pltpu.roll(jnp.where(mask, b, a), 8 - shift, 0)

    def half(offset):
        return ((sub + (8 - offset)) % 8) < 4

    def quarter(offset):
        return ((sub + (8 - offset)) % 4) < 2

    z1 = join(
        join(vregs[0], vregs[4], half(0), 4), join(vregs[2], vregs[6], half(2), 4), quarter(0), 2
    )
    z2 = join(
        join(vregs[1], vregs[5], half(1), 4), join(vregs[3], vregs[7], half(3), 4), quarter(1), 2
    )
    return join(z1, z2, (sub % 2) < 1, 1)


def step_kernel(
    geometry,
    table_ref,
    target_ref,
    gauss_ref,
    across_ref,
    first_ref,
    second_ref,
    power_ref,
    incoming_ref,
    messages_ref,
    msg_in,
    rec_out,
    rec_in,
    grad_out,
    grad_in,
    halo_out,
    halo_in,
    thalo_out,
    thalo_in,
    coef,
    alpha_s,
    trans_s,
    moment_s,
    send_sem,
    recv_sem,
    halo_send,
    halo_recv,
):
    views_n, bands_n, blocks, list_len, rows, cols, block_len = geometry
    devices = views_n * bands_n
    tiles = cols // TILE
    pairs = TILE_MOST * tiles
    window = TILE_MOST * block_len
    halves = block_len // 128
    view = lax.axis_index("view")
    band = lax.axis_index("band")
    me = view * bands_n + band
    base = (me * blocks).astype(F32)
    has_up = band > 0
    has_down = band < bands_n - 1

    def peer_of(d):
        peer = lax.rem(me + d, devices)
        return (peer // bands_n, lax.rem(peer, bands_n))

    halo_in[...] = jnp.zeros_like(halo_in)
    thalo_in[...] = jnp.zeros_like(thalo_in)
    thalo_out[0] = target_ref[0, :, 0:REACH, :]
    thalo_out[1] = target_ref[0, :, rows - REACH : rows, :]
    barrier = pltpu.get_barrier_semaphore()

    def greet(d, carry):
        pl.semaphore_signal(barrier, inc=1, device_id=peer_of(d), device_id_type=MESH)
        return carry

    lax.fori_loop(1, devices, greet, 0)
    pl.semaphore_wait(barrier, devices - 1)

    def to_all(source_of, landing, phase):
        def send(d, carry):
            peer = lax.rem(me + d, devices)
            pltpu.make_async_remote_copy(
                src_ref=source_of(peer),
                dst_ref=landing.at[me],
                send_sem=send_sem.at[phase],
                recv_sem=recv_sem.at[phase],
                device_id=peer_of(d),
                device_id_type=MESH,
            ).start()
            return carry

        lax.fori_loop(1, devices, send, 0)

    def wait_all(landing, phase):
        every = landing.at[pl.ds(0, devices - 1)]
        pltpu.make_async_copy(every, every, recv_sem.at[phase]).wait()
        pltpu.make_async_copy(every, every, send_sem.at[phase]).wait()

    def edge_copy(source, landing, direction, phase):
        step = -1 if direction == 0 else 1
        return pltpu.make_async_remote_copy(
            src_ref=source.at[direction],
            dst_ref=landing.at[1 - direction],
            send_sem=halo_send.at[phase, direction],
            recv_sem=halo_recv.at[phase, 1 - direction],
            device_id=(view, band + step),
            device_id_type=MESH,
        )

    def edges_start(source, landing, phase):
        @pl.when(has_up)
        def _():
            edge_copy(source, landing, 0, phase).start()

        @pl.when(has_down)
        def _():
            edge_copy(source, landing, 1, phase).start()

    def edges_wait(source, landing, phase):
        @pl.when(has_up)
        def _():
            up = edge_copy(source, landing, 0, phase)
            up.wait_send()
            pltpu.make_async_copy(
                landing.at[0], landing.at[0], halo_recv.at[phase, 0]
            ).wait()

        @pl.when(has_down)
        def _():
            down = edge_copy(source, landing, 1, phase)
            down.wait_send()
            pltpu.make_async_copy(
                landing.at[1], landing.at[1], halo_recv.at[phase, 1]
            ).wait()

    message = table_ref.at[0]
    to_all(lambda peer: message, msg_in, 0)
    edges_start(thalo_out, thalo_in, 0)
    msg_in[me] = table_ref[0]

    list_row = table_ref[0][:, 16 : 16 + list_len]
    owner_low = lax.broadcasted_iota(jnp.int32, (devices, list_len), 0).astype(F32) * blocks
    owner_hot = jnp.where((list_row >= owner_low) & (list_row < owner_low + blocks), 1.0, 0.0)
    place = jnp.concatenate(
        [table_ref[1 + pair][:, 0:list_len] for pair in range(pairs)], axis=0
    )
    live_pair = jnp.max(place, axis=1, keepdims=True)
    pick_owner = lax.dot_general(
        place.astype(BF16), owner_hot.astype(BF16), (NT, ((), ())), preferred_element_type=F32
    )
    put_owner = lax.dot_general(
        owner_hot.astype(BF16), place.astype(BF16), (NT, ((), ())), preferred_element_type=F32
    )
    live = jnp.concatenate(
        [
            jnp.broadcast_to(live_pair[k * tiles : (k + 1) * tiles], (tiles, block_len))
            for k in range(TILE_MOST)
        ],
        axis=1,
    )

    wait_all(msg_in, 0)

    asked = msg_in[...].reshape(devices, 128)
    messages_ref[...] = asked
    hot = requests_of(asked, base, list_len, blocks)
    missing = 1.0 - jnp.max(hot, axis=1, keepdims=True)
    cam = [asked[:, c : c + 1] for c in range(9)]

    def picked(component):
        return exact_dot(hot, gauss_ref[:, component, :], NN)

    centre = [picked(c) + cam[8] * picked(3 + c) for c in range(3)]
    records = [
        cam[0] * centre[0] + cam[1] * centre[1] + cam[2] * centre[2] + cam[6],
        cam[3] * centre[0] + cam[4] * centre[1] + cam[5] * centre[2] + cam[7],
    ]
    quats = [picked(9 + c) for c in range(4)]
    quats[0] = quats[0] + missing
    conic_a, conic_b, conic_c, opacity = shape_of(
        cam[0:6], [picked(6 + c) for c in range(3)], quats, picked(13)
    )
    records += [conic_a, conic_b, conic_c, opacity]
    basis = camera_basis(cam)
    basis = [jnp.where(missing > 0.5, 0.0, value) for value in basis]
    for ch in range(3):
        colour = 0.5
        for q in range(16):
            colour = colour + basis[q] * picked(14 + 3 * q + ch)
        records.append(colour)
    for p in range(ROW_REC):
        for h in range(halves):
            rec_out[:, p * halves + h, :] = records[p][:, h * 128 : (h + 1) * 128]
    to_all(lambda peer: rec_out.at[peer], rec_in, 1)
    rec_in[me] = rec_out[me]
    wait_all(rec_in, 1)

    def gathered(p):
        parts = []
        for h in range(halves):
            parts.append(exact_dot(pick_owner, rec_in[:, p * halves + h, :], NN))
        whole = jnp.concatenate(parts, axis=1)
        return jnp.concatenate(
            [whole[k * tiles : (k + 1) * tiles] for k in range(TILE_MOST)], axis=1
        )

    dead = 1.0 - live
    tile_row = lax.broadcasted_iota(jnp.int32, (tiles, window), 0).astype(F32)
    u_rel = gathered(0) - (tile_row * TILE + 0.5 * TILE)
    w_rel = gathered(1) - ((band * rows).astype(F32) + 0.5 * TILE)
    c_a = gathered(2) + dead
    c_b = gathered(3)
    c_c = gathered(4) + dead
    opac = gathered(5) + dead
    inv_det = 1.0 / (c_a * c_c - c_b * c_b)
    coef_a = -0.5 * c_c * inv_det
    coef_b = c_b * inv_det
    coef_c = -0.5 * c_a * inv_det
    keep = live > 0.5

    def masked(value, other=0.0):
        return jnp.where(keep, value, other)

    flat = LOG2_E * (
        coef_a * u_rel * u_rel + coef_b * u_rel * w_rel + coef_c * w_rel * w_rel
    ) + LOG2_E * jnp.log(opac)
    power = power_ref[...]
    coef[0] = expand_dot(
        jnp.concatenate(
            [
                masked(flat, NEVER),
                masked(LOG2_E * (-2.0 * coef_a * u_rel - coef_b * w_rel)),
                masked(LOG2_E * coef_a),
            ],
            axis=0,
        ),
        power,
    )
    coef[1] = expand_dot(
        jnp.concatenate(
            [
                masked(LOG2_E * (-coef_b * u_rel - 2.0 * coef_c * w_rel)),
                masked(LOG2_E * coef_b),
            ],
            axis=0,
        ),
        power[0 : 2 * tiles],
    )
    coef[2] = expand_dot(masked(LOG2_E * coef_c), power[0:tiles])
    for ch in range(3):
        coef[3 + ch] = expand_dot(masked(gathered(6 + ch)), power[0:tiles])

    sub8 = lax.broadcasted_iota(jnp.int32, (8, cols), 0).astype(F32)
    parts_n = rows // 8
    row_local = [sub8 + (8.0 * part + 0.5 - 0.5 * TILE) for part in range(parts_n)]

    def spread_row(kind, j):
        return coef[kind, pl.ds(j, 8, stride=0), :]

    def blend(group, carry):
        trans, image = carry
        trans, image = list(trans), list(image)
        for k in range(8):
            j = group * 8 + k
            q0, q1, q2 = spread_row(0, j), spread_row(1, j), spread_row(2, j)
            tint = [spread_row(3 + ch, j) for ch in range(3)]
            for part in range(parts_n):
                r = row_local[part]
                alpha = jnp.exp2(q0 + r * (q1 + r * q2))
                weight = alpha * trans[part]
                alpha_s[j, part] = alpha
                trans_s[j, part] = trans[part]
                trans[part] = trans[part] - weight
                for ch in range(3):
                    at = ch * parts_n + part
                    image[at] = image[at] + weight * tint[ch]
        return tuple(trans), tuple(image)

    zero = jnp.zeros((8, cols), F32)
    _, image = lax.fori_loop(
        0,
        window // 8,
        blend,
        (tuple([zero + 1.0] * parts_n), tuple([zero] * (3 * parts_n))),
    )
    pred = [
        jnp.concatenate([image[ch * parts_n + part] for part in range(parts_n)], axis=0)
        for ch in range(3)
    ]
    for ch in range(3):
        halo_out[0, ch] = pred[ch][0:REACH]
        halo_out[1, ch] = pred[ch][rows - REACH : rows]
    edges_start(halo_out, halo_in, 1)
    edges_wait(thalo_out, thalo_in, 0)
    edges_wait(halo_out, halo_in, 1)

    in_rows, mid_rows = up8(rows + 2 * REACH), up8(rows + REACH)
    fill = jnp.zeros((in_rows - rows - 2 * REACH, cols), F32)
    mine = target_ref[0]
    ext_x = jnp.concatenate(
        [v for ch in range(3) for v in (halo_in[0, ch], pred[ch], halo_in[1, ch], fill)], axis=0
    )
    ext_y = jnp.concatenate(
        [v for ch in range(3) for v in (thalo_in[0, ch], mine[ch], thalo_in[1, ch], fill)], axis=0
    )
    fields = jnp.concatenate(
        [ext_x, ext_y, ext_x * ext_x, ext_y * ext_y, ext_x * ext_y], axis=1
    )
    down = jnp.dot(first_ref[...], fields, precision=HIGHEST_MODE, preferred_element_type=F32)
    stacked = jnp.concatenate([down[:, f * cols : (f + 1) * cols] for f in range(5)], axis=0)
    smoothed = jnp.dot(
        stacked, across_ref[...], precision=HIGHEST_MODE, preferred_element_type=F32
    )
    high = 3 * mid_rows
    mean_x, mean_y, square_x, square_y, cross = [
        smoothed[f * high : (f + 1) * high] for f in range(5)
    ]
    n_mean = 2.0 * mean_x * mean_y + STAB_MEAN
    n_var = 2.0 * (cross - mean_x * mean_y) + STAB_VAR
    d_mean = mean_x * mean_x + mean_y * mean_y + STAB_MEAN
    d_var = (square_x - mean_x * mean_x) + (square_y - mean_y * mean_y) + STAB_VAR
    inv_mean = 1.0 / d_mean
    inv_var = 1.0 / d_var
    inverse = inv_mean * inv_var
    ssim = n_mean * n_var * inverse
    ext_row = lax.broadcasted_iota(jnp.int32, (high, cols), 0) % mid_rows
    image_row = ext_row + (band * rows - HALO)
    inside = (image_row >= 0) & (image_row < bands_n * rows) & (ext_row < rows + REACH)
    scale = -SSIM_WEIGHT / 3.0
    part_mean = 2.0 * mean_y * (n_var - n_mean) * inverse - 2.0 * mean_x * ssim * (
        inv_mean - inv_var
    )
    adjoint = jnp.concatenate(
        [
            jnp.where(inside, scale * part_mean, 0.0),
            jnp.where(inside, -scale * ssim * inv_var, 0.0),
            jnp.where(inside, (2.0 * scale) * n_mean * inverse, 0.0),
        ],
        axis=1,
    )
    down2 = jnp.dot(second_ref[...], adjoint, precision=HIGHEST_MODE, preferred_element_type=F32)
    stacked2 = jnp.concatenate([down2[:, f * cols : (f + 1) * cols] for f in range(3)], axis=0)
    spread = jnp.dot(
        stacked2, across_ref[...], precision=HIGHEST_MODE, preferred_element_type=F32
    )
    deep = 3 * rows
    pred_all = jnp.concatenate(pred, axis=0)
    mine_all = jnp.concatenate([mine[ch] for ch in range(3)], axis=0)
    error = pred_all - mine_all
    sign = jnp.where(error > 0.0, 1.0, jnp.where(error < 0.0, -1.0, 0.0))
    grad_pred = (
        ABS_WEIGHT / 3.0 * sign
        + spread[0:deep]
        + 2.0 * pred_all * spread[deep : 2 * deep]
        + mine_all * spread[2 * deep : 3 * deep]
    )
    own = (ext_row >= HALO) & (ext_row < HALO + rows)
    loss = jnp.sum(ABS_WEIGHT / 3.0 * jnp.abs(error), keepdims=True) + jnp.sum(
        jnp.where(own, SSIM_WEIGHT / 3.0 * (1.0 - ssim), 0.0), keepdims=True
    )

    pull = [
        [grad_pred[ch * rows + 8 * part : ch * rows + 8 * part + 8] for part in range(parts_n)]
        for ch in range(3)
    ]

    def unblend(step, behind):
        group = window // 8 - 1 - step
        behind = list(behind)
        sums = [[None] * 8 for _ in range(6)]
        for k in reversed(range(8)):
            j = group * 8 + k
            tint = [spread_row(3 + ch, j) for ch in range(3)]
            totals = [None] * 6
            for part in range(parts_n):
                alpha = alpha_s[j, part]
                trans = trans_s[j, part]
                shade = (
                    tint[0] * pull[0][part] + tint[1] * pull[1][part] + tint[2] * pull[2][part]
                )
                gap = shade - behind[part]
                behind[part] = behind[part] + alpha * gap
                weight = alpha * trans
                lean = weight * gap
                lean_r = lean * row_local[part]
                terms = [lean, lean_r, lean_r * row_local[part]]
                terms += [weight * pull[ch][part] for ch in range(3)]
                totals = [
                    term if total is None else total + term for term, total in zip(terms, totals)
                ]
            for kind in range(6):
                sums[kind][k] = totals[kind]
        at = pl.multiple_of(group * 8, 8)
        for kind in range(6):
            moment_s[kind, pl.ds(at, 8), :] = tree_sum(sums[kind], cols)
        return tuple(behind)

    lax.fori_loop(0, window // 8, unblend, tuple([zero] * parts_n))

    by_x = exact_dot(power, moment_s[0], NT)
    m_00, m_10, m_20 = by_x[0:tiles], by_x[tiles : 2 * tiles], by_x[2 * tiles : 3 * tiles]
    by_xr = exact_dot(power[0 : 2 * tiles], moment_s[1], NT)
    m_01, m_11 = by_xr[0:tiles], by_xr[tiles : 2 * tiles]
    m_02 = exact_dot(power[0:tiles], moment_s[2], NT)
    s_x = m_10 - u_rel * m_00
    s_y = m_01 - w_rel * m_00
    s_xx = m_20 - 2.0 * u_rel * m_10 + u_rel * u_rel * m_00
    s_xy = m_11 - u_rel * m_01 - w_rel * m_10 + u_rel * w_rel * m_00
    s_yy = m_02 - 2.0 * w_rel * m_01 + w_rel * w_rel * m_00
    by_det = -(coef_a * s_xx + coef_b * s_xy + coef_c * s_yy) * inv_det
    derivs = [
        -(2.0 * coef_a * s_x + coef_b * s_y),
        -(2.0 * coef_c * s_y + coef_b * s_x),
        -0.5 * inv_det * s_yy + by_det * c_c,
        inv_det * s_xy - 2.0 * c_b * by_det,
        -0.5 * inv_det * s_xx + by_det * c_a,
        m_00 / opac,
    ] + [exact_dot(power[0:tiles], moment_s[3 + ch], NT) for ch in range(3)]
    for p in range(ROW_REC):
        split_pairs = jnp.concatenate(
            [derivs[p][:, k * block_len : (k + 1) * block_len] for k in range(TILE_MOST)], axis=0
        )
        routed = exact_dot(put_owner, split_pairs, NN)
        for h in range(halves):
            grad_out[:, p * halves + h, :] = routed[:, h * 128 : (h + 1) * 128]
    grad_out[:, ROW_REC * halves, :] = jnp.broadcast_to(loss, (devices, 128))
    to_all(lambda peer: grad_out.at[peer], grad_in, 2)
    grad_in[me] = grad_out[me]
    wait_all(grad_in, 2)
    incoming_ref[...] = grad_in[...]


def adam_kernel(
    geometry,
    messages_ref,
    incoming_ref,
    rates_ref,
    gauss_ref,
    one_ref,
    two_ref,
    out_gauss,
    out_one,
    out_two,
    out_loss,
    out_grad,
):
    views_n, bands_n, blocks, list_len, rows, cols, block_len = geometry
    devices = views_n * bands_n
    halves = block_len // 128
    me = lax.axis_index("view") * bands_n + lax.axis_index("band")
    base = (me * blocks).astype(F32)
    asked = messages_ref[...]
    hot = requests_of(asked, base, list_len, blocks)
    missing = 1.0 - jnp.max(hot, axis=1, keepdims=True)
    cam = [asked[:, c : c + 1] for c in range(9)]

    def picked(component):
        return exact_dot(hot, gauss_ref[:, component, :], NN)

    def arrived(p):
        return jnp.concatenate(
            [incoming_ref[:, p * halves + h, :] for h in range(halves)], axis=1
        )

    d_u, d_w = arrived(0), arrived(1)
    columns = []
    along = [cam[c] * d_u + cam[3 + c] * d_w for c in range(3)]
    columns += along + [cam[8] * value for value in along]
    quats = [picked(9 + c) for c in range(4)]
    quats[0] = quats[0] + missing
    logs = [picked(6 + c) for c in range(3)]
    _, pullback = jax.vjp(
        lambda a, b, c: shape_of(cam[0:6], a, b, c), logs, quats, picked(13)
    )
    d_logs, d_quats, d_logit = pullback(tuple(arrived(2 + p) for p in range(4)))
    columns += list(d_logs) + list(d_quats) + [d_logit]
    turned = jnp.transpose(jnp.concatenate([asked] * 3, axis=0))
    hot_t = jnp.transpose(hot)
    for c in range(14):
        out_grad[:, c, :] = exact_dot(hot_t, columns[c], NN)
    basis = camera_basis([turned[c : c + 1, :] for c in range(6)])
    channel = lax.broadcasted_iota(jnp.int32, (3, 3 * devices), 1) // devices
    own_channel = channel == lax.broadcasted_iota(jnp.int32, (3, 3 * devices), 0)
    fan = jnp.concatenate([jnp.where(own_channel, value, 0.0) for value in basis], axis=0)
    hot_3 = jnp.transpose(jnp.concatenate([hot] * 3, axis=0))
    routed = jnp.concatenate([hot_3[b : b + 1, :] * fan for b in range(blocks)], axis=0)
    tinted = jnp.concatenate([arrived(6 + ch) for ch in range(3)], axis=0)
    colour = jnp.dot(routed, tinted, precision=HIGHEST_MODE, preferred_element_type=F32)
    shades = fan.shape[0]
    for b in range(blocks):
        out_grad[b, 14:, :] = colour[b * shades : (b + 1) * shades]
    losses = incoming_ref[:, ROW_REC * halves, :]
    out_loss[...] = jnp.sum(losses, axis=0, keepdims=True)[:, 0:1] * (
        1.0 / (devices * rows * cols)
    )
    rates = rates_ref[...]

    def update(b, carry):
        gradient = out_grad[b]
        new_one = 0.9 * one_ref[b] + 0.1 * gradient
        new_two = 0.999 * two_ref[b] + 0.001 * gradient * gradient
        out_one[b] = new_one
        out_two[b] = new_two
        change = rates * (new_one / BIAS_FIRST) / (jnp.sqrt(new_two / BIAS_SECOND) + 1e-08)
        out_gauss[b] = gauss_ref[b] - change
        return carry

    lax.fori_loop(0, blocks, update, 0)


def per_device(
    gaussians,
    first_moment,
    second_moment,
    camera,
    target,
    block_list,
    block_count,
    tile_start,
    tile_end,
):
    views_n = lax.axis_size("view")
    bands_n = lax.axis_size("band")
    devices = views_n * bands_n
    blocks, comps, block_len = gaussians.shape
    list_len = block_list.shape[2]
    rows, cols = target.shape[2:]
    tiles = cols // TILE
    pairs = TILE_MOST * tiles
    halves = block_len // 128
    geometry = (views_n, bands_n, blocks, list_len, rows, cols, block_len)

    message = jnp.concatenate(
        [
            camera,
            jnp.zeros((1, 7), F32),
            block_list[0].astype(F32),
            jnp.zeros((1, 128 - 16 - list_len), F32),
        ],
        axis=1,
    )
    spot = tile_start[0, 0][None, :] + jnp.arange(TILE_MOST, dtype=jnp.int32)[:, None]
    spot = jnp.where(spot < tile_end[0, 0][None, :], spot, -1).reshape(pairs, 1)
    place = (spot == jnp.arange(128, dtype=jnp.int32)[None, :]).astype(F32)
    table = jnp.concatenate([message, place], axis=0)[:, None, :]

    across, first, second = smoothing_tables(rows, cols, 3)
    power = power_table(tiles, cols)
    vmem = pl.BlockSpec(memory_space=pltpu.VMEM)
    rec_rows = ROW_REC * halves
    window = TILE_MOST * block_len
    incoming, messages = pl.pallas_call(
        functools.partial(step_kernel, geometry),
        out_shape=(
            jax.ShapeDtypeStruct((devices, rec_rows + 1, 128), F32),
            jax.ShapeDtypeStruct((devices, 128), F32),
        ),
        in_specs=[vmem] * 7,
        out_specs=(vmem, vmem),
        scratch_shapes=[
            pltpu.VMEM((devices, 1, 128), F32),
            pltpu.VMEM((devices, rec_rows, 128), F32),
            pltpu.VMEM((devices, rec_rows, 128), F32),
            pltpu.VMEM((devices, rec_rows + 1, 128), F32),
            pltpu.VMEM((devices, rec_rows + 1, 128), F32),
            pltpu.VMEM((2, 3, REACH, cols), F32),
            pltpu.VMEM((2, 3, REACH, cols), F32),
            pltpu.VMEM((2, 3, REACH, cols), F32),
            pltpu.VMEM((2, 3, REACH, cols), F32),
            pltpu.VMEM((6, window, cols), F32),
            pltpu.VMEM((window, rows // 8, 8, cols), F32),
            pltpu.VMEM((window, rows // 8, 8, cols), F32),
            pltpu.VMEM((6, window, cols), F32),
            pltpu.SemaphoreType.DMA((3,)),
            pltpu.SemaphoreType.DMA((3,)),
            pltpu.SemaphoreType.DMA((2, 2)),
            pltpu.SemaphoreType.DMA((2, 2)),
        ],
        compiler_params=pltpu.CompilerParams(collective_id=0, has_side_effects=True),
        name="render_step",
    )(table, target, gaussians, across, first, second, power)

    rates = np.ascontiguousarray(np.broadcast_to(learning_rates()[:, None], (comps, block_len)))
    shape = jax.ShapeDtypeStruct(gaussians.shape, F32)
    new_params, new_one, new_two, mean_loss, gradient = pl.pallas_call(
        functools.partial(adam_kernel, geometry),
        out_shape=(shape, shape, shape, jax.ShapeDtypeStruct((1, 1), F32), shape),
        in_specs=[vmem] * 6,
        out_specs=(vmem,) * 5,
        name="adam_step",
    )(messages, incoming, rates, gaussians, first_moment, second_moment)
    return (new_params, new_one, new_two, mean_loss.reshape(()), gradient)


def solution(mesh):
    return jax.shard_map(
        per_device,
        mesh=mesh,
        in_specs=(
            P(("view", "band"), None, None),
            P(("view", "band"), None, None),
            P(("view", "band"), None, None),
            P("view", None),
            P("view", None, "band", None),
            P("view", "band", None),
            P("view", "band"),
            P("view", "band", None),
            P("view", "band", None),
        ),
        out_specs=(
            P(("view", "band"), None, None),
            P(("view", "band"), None, None),
            P(("view", "band"), None, None),
            P(),
            P(("view", "band"), None, None),
        ),
        check_vma=False,
    )
```

time: 410 us -> 76.8 us (0.19)
  other arithmetic: 145 us -> 0.17 us
  loops' own time: 78 us -> 0 us
  Pallas kernels: 0 us -> 58.9 us
  blocking collectives: 50.1 us -> 0 us
  local copies, waits for them, and re-layouts: 58 us -> 16.8 us
  matrix products: 26.2 us -> 0 us
  starting transfers between devices: 23.6 us -> 0 us
  waiting for transfers between devices: 22.9 us -> 0 us
    another operation x2 -> x0, loops' own time: 78 us -> none  [the longest x1 39.4 us: backward_band(): lax.scan(tile_back, jnp.zeros_like(listed), jnp.arange(starts.shape[0], d...]
    another operation x99 -> x0, other arithmetic: 76.4 us -> none
    pallas_call x0 -> x2, Pallas kernels: none -> 58.9 us  [the longest x1 51.8 us: per_device(): pl.pallas_call(functools.partial(step_kernel, geometry), out_shape=(jax.S...]
    psum x1 -> x0, blocking collectives: 41 us -> none  [per_device(): loss_sum = lax.psum(local_loss, ('view', 'band'))]
    dynamic_slice x56 -> x0, local copies, waits for them, and re-layouts: 28.2 us -> none  [the longest x16 9.39 us: tile_frame(): starts[tile_index]]
    dot_general x29 -> x0, matrix products: 26.2 us -> none  [the longest x24 14.9 us: blend_tile(): return jnp.dot(colour.reshape(3, -1), weight, precision=HIGHEST_MODE)]
    mul x41 -> x0, other arithmetic: 22.5 us -> none  [the longest x16 12 us: blend_tile(): weight = alphas * jnp.exp(log_trans.reshape(window_len * block_len, -1))]
    and x17 -> x0, other arithmetic: 20.8 us -> none  [the longest x16 20.8 us: blend_tile(): is_live = (positions >= live_low) & (positions < live_high)]
  transfers between devices with their start and end apart: 7 -> 0, of which waited for: 5 -> 0; matrix products, arithmetic and copies ran while one was open for 0% -> 0% of each run, Pallas kernels for 0% -> 0%
where the time goes in v1:
time: 76.8 us; the launch traced here: 76.5 us
  Pallas kernels  58.9 us (77%)
  local copies, waits for them, and re-layouts  16.8 us (22%)
    pallas_call x1, Pallas kernels, per_device(): pl.pallas_call(functools.partial(step_kernel, geometry), out_shape=(jax.S...  51.8 us
    unnamed x25, local copies, waits for them, and re-layouts  16 us
    pallas_call x1, Pallas kernels, per_device(): pl.pallas_call(functools.partial(adam_kernel, geometry), out_shape=(shape...  7.12 us

profile of v1, /device:TPU:0, one launch (start us, length us, event | category | flops | bytes accessed | tf_op | source)
XLA Modules:
  0.0 76.5 jit_solution(7287138680940409787)
XLA Ops:
  0.6 0.0 copy-start.6
  0.6 0.6 copy-done.6
  1.3 0.7 copy-done.7
  2.0 0.1 add.26
  2.0 0.6 copy-done.8
  2.6 0.1 lt.18
  2.7 0.1 fusion
  2.8 0.6 copy-done.5
  3.4 0.1 pad_maximum_fusion
  3.5 0.6 broadcast_in_dim.14.table_ref
  4.1 2.8 %copy.18.gauss_ref = f32[16,62,256]{2,1,0:T(8,128)} copy(f32[16,62,256]{2,0,1:T(8,128)} %param.14) | data formatting | bytes 2031616 | tf_op args[0]
  6.9 51.8 %render_step.1 = (f32[32,19,128]{2,1,0:T(8,128)}, f32[32,128]{1,0:T(8,128)}) custom-call(f32[17,1,128]{2,1,0:T(1,128)} %broadcast_in_dim.14.table_ref, f32[1,3,16,128]{3,2,1,0:T(8,128)} %target_ref.1, f32[16,62,256]{2,1,0:T(8,128)} %copy.18.gauss_ref, f32[128,128]{1,0:T(8,128)} %constant.6.clone.across_ref, f32[96,120]{1,0:T(8,128)} %constant.16.clone.first_ref, ...), custom_call_target="tpu_custom_call" | custom-call | tf_op jit(solution)/shard_map/render_step/pallas_call | solution.py:756
  58.7 0.0 copy-done.3
  58.7 0.0 copy-start.4
  58.7 1.6 %copy.20.one_ref = f32[16,62,256]{2,1,0:T(8,128)} copy(f32[16,62,256]{2,0,1:T(8,128)S(1)} %copy-done.3) | data formatting | bytes 2031616 | tf_op args[1]
  60.3 0.0 copy-done.4
  60.3 1.6 %copy.21.two_ref = f32[16,62,256]{2,1,0:T(8,128)} copy(f32[16,62,256]{2,0,1:T(8,128)S(1)} %copy-done.4) | data formatting | bytes 2031616 | tf_op args[2]
  61.9 7.1 %adam_step.1 = (f32[16,62,256]{2,1,0:T(8,128)}, f32[16,62,256]{2,1,0:T(8,128)}, f32[16,62,256]{2,1,0:T(8,128)}, f32[1,1]{1,0:T(1,128)}, f32[16,62,256]{2,1,0:T(8,128)}) custom-call(f32[32,128]{1,0:T(8,128)} %get-tuple-element.12.messages_ref, f32[32,19,128]{2,1,0:T(8,128)} %get-tuple-element.13.incoming_ref, f32[62,256]{1,0:T(8,128)} %constant.19.clone.rates_ref, ...), custom_call_target="tpu_custom_call" | custom-call | tf_op jit(solution)/shard_map/adam_step/pallas_call | solution.py:789
  69.0 2.9 %copy.22 = f32[16,62,256]{2,0,1:T(8,128)} copy(f32[16,62,256]{2,1,0:T(8,128)} %get-tuple-element.19) | data formatting | bytes 2031616
  71.9 0.0 copy-done.2
  71.9 1.5 %copy.23 = f32[16,62,256]{2,0,1:T(8,128)} copy(f32[16,62,256]{2,1,0:T(8,128)S(1)} %copy-done.2) | data formatting | bytes 2031616
  73.4 1.5 %copy.24 = f32[16,62,256]{2,0,1:T(8,128)} copy(f32[16,62,256]{2,1,0:T(8,128)S(1)} %copy-done.1) | data formatting | bytes 2031616
  75.0 0.0 copy-done
  75.0 1.5 %copy.25 = f32[16,62,256]{2,0,1:T(8,128)} copy(f32[16,62,256]{2,1,0:T(8,128)S(1)} %copy-done) | data formatting | bytes 2031616
  (14 shorter events, 0.0 us)
Async XLA Ops:
  0.6 0.7 copy-start.6
  1.3 0.7 copy-start.7
  1.9 0.7 copy-start.8
  2.8 0.7 copy-start.5
  6.9 51.8 %copy-start.3 = (f32[16,62,256]{2,0,1:T(8,128)S(1)}, f32[16,62,256]{2,0,1:T(8,128)}, u32[]{:S(2)}) copy-start(f32[16,62,256]{2,0,1:T(8,128)} %param.15) | copy-start | bytes 3047428
  58.7 1.6 %copy-start.4 = (f32[16,62,256]{2,0,1:T(8,128)S(1)}, f32[16,62,256]{2,0,1:T(8,128)}, u32[]{:S(2)}) copy-start(f32[16,62,256]{2,0,1:T(8,128)} %param.16) | copy-start | bytes 3047428
  69.0 2.9 %copy-start.2 = (f32[16,62,256]{2,1,0:T(8,128)S(1)}, f32[16,62,256]{2,1,0:T(8,128)}, u32[]{:S(2)}) copy-start(f32[16,62,256]{2,1,0:T(8,128)} %get-tuple-element.20) | copy-start | bytes 3047428
  71.9 1.6 %copy-start.1 = (f32[16,62,256]{2,1,0:T(8,128)S(1)}, f32[16,62,256]{2,1,0:T(8,128)}, u32[]{:S(2)}) copy-start(f32[16,62,256]{2,1,0:T(8,128)} %get-tuple-element.21) | copy-start | bytes 3047428
  73.4 1.6 %copy-start = (f32[16,62,256]{2,1,0:T(8,128)S(1)}, f32[16,62,256]{2,1,0:T(8,128)}, u32[]{:S(2)}) copy-start(f32[16,62,256]{2,1,0:T(8,128)} %get-tuple-element.23) | copy-start | bytes 3047428

commit v2 on v1

--- a/solution.py
+++ b/solution.py
@@ -14,6 +14,7 @@
 HALO = 5
 REACH = 2 * HALO
 ROW_REC = 9
+PIECES = 4
 
 HIGHEST_MODE = lax.Precision.HIGHEST
 SSIM_WEIGHT = 0.2
@@ -372,7 +373,7 @@
     cam = [asked[:, c : c + 1] for c in range(9)]
 
     def picked(component):
-        return exact_dot(hot, gauss_ref[:, component, :], NN)
+        return exact_dot(hot, gauss_ref[component], NN)
 
     centre = [picked(c) + cam[8] * picked(3 + c) for c in range(3)]
     records = [
@@ -646,8 +647,18 @@
     out_one,
     out_two,
     out_loss,
+    out_grad_hbm,
     out_grad,
+    one_v,
+    two_v,
+    gauss_v,
+    read_sem,
+    write_sem,
 ):
+    fetch_one = pltpu.make_async_copy(one_ref, one_v, read_sem.at[0])
+    fetch_two = pltpu.make_async_copy(two_ref, two_v, read_sem.at[1])
+    fetch_one.start()
+    fetch_two.start()
     views_n, bands_n, blocks, list_len, rows, cols, block_len = geometry
     devices = views_n * bands_n
     halves = block_len // 128
@@ -659,7 +670,7 @@
     cam = [asked[:, c : c + 1] for c in range(9)]
 
     def picked(component):
-        return exact_dot(hot, gauss_ref[:, component, :], NN)
+        return exact_dot(hot, gauss_ref[component], NN)
 
     def arrived(p):
         return jnp.concatenate(
@@ -681,35 +692,54 @@
     turned = jnp.transpose(jnp.concatenate([asked] * 3, axis=0))
     hot_t = jnp.transpose(hot)
     for c in range(14):
-        out_grad[:, c, :] = exact_dot(hot_t, columns[c], NN)
+        out_grad[c] = exact_dot(hot_t, columns[c], NN)
     basis = camera_basis([turned[c : c + 1, :] for c in range(6)])
     channel = lax.broadcasted_iota(jnp.int32, (3, 3 * devices), 1) // devices
     own_channel = channel == lax.broadcasted_iota(jnp.int32, (3, 3 * devices), 0)
     fan = jnp.concatenate([jnp.where(own_channel, value, 0.0) for value in basis], axis=0)
     hot_3 = jnp.transpose(jnp.concatenate([hot] * 3, axis=0))
-    routed = jnp.concatenate([hot_3[b : b + 1, :] * fan for b in range(blocks)], axis=0)
+    shades = fan.shape[0]
+    routed = jnp.concatenate([hot_3 * fan[r : r + 1, :] for r in range(shades)], axis=0)
     tinted = jnp.concatenate([arrived(6 + ch) for ch in range(3)], axis=0)
     colour = jnp.dot(routed, tinted, precision=HIGHEST_MODE, preferred_element_type=F32)
-    shades = fan.shape[0]
-    for b in range(blocks):
-        out_grad[b, 14:, :] = colour[b * shades : (b + 1) * shades]
+    for r in range(shades):
+        out_grad[14 + r] = colour[r * blocks : (r + 1) * blocks]
     losses = incoming_ref[:, ROW_REC * halves, :]
     out_loss[...] = jnp.sum(losses, axis=0, keepdims=True)[:, 0:1] * (
         1.0 / (devices * rows * cols)
     )
-    rates = rates_ref[...]
-
-    def update(b, carry):
-        gradient = out_grad[b]
-        new_one = 0.9 * one_ref[b] + 0.1 * gradient
-        new_two = 0.999 * two_ref[b] + 0.001 * gradient * gradient
-        out_one[b] = new_one
-        out_two[b] = new_two
-        change = rates * (new_one / BIAS_FIRST) / (jnp.sqrt(new_two / BIAS_SECOND) + 1e-08)
-        out_gauss[b] = gauss_ref[b] - change
-        return carry
-
-    lax.fori_loop(0, blocks, update, 0)
+    fetch_one.wait()
+    fetch_two.wait()
+    comps = gauss_ref.shape[0]
+    pieces = []
+    for piece in range(PIECES):
+        low, high = piece * comps // PIECES, (piece + 1) * comps // PIECES
+
+        def update(c, carry):
+            gradient = out_grad[c]
+            new_one = 0.9 * one_v[c] + 0.1 * gradient
+            new_two = 0.999 * two_v[c] + 0.001 * gradient * gradient
+            one_v[c] = new_one
+            two_v[c] = new_two
+            bottom = jnp.sqrt(new_two * (1.0 / BIAS_SECOND)) + 1e-08
+            gauss_v[c] = gauss_ref[c] - rates_ref[c] * new_one / bottom
+            return carry
+
+        lax.fori_loop(low, high, update, 0, unroll=2)
+        part = pl.ds(low, high - low)
+        for source, landing, sem in (
+            (one_v, out_one, 0),
+            (two_v, out_two, 1),
+            (gauss_v, out_gauss, 2),
+            (out_grad, out_grad_hbm, 3),
+        ):
+            copy = pltpu.make_async_copy(
+                source.at[part], landing.at[part], write_sem.at[sem, piece]
+            )
+            copy.start()
+            pieces.append(copy)
+    for copy in pieces:
+        copy.wait()
 
 
 def per_device(
@@ -751,6 +781,11 @@
     across, first, second = smoothing_tables(rows, cols, 3)
     power = power_table(tiles, cols)
     vmem = pl.BlockSpec(memory_space=pltpu.VMEM)
+    hbm = pl.BlockSpec(memory_space=pl.ANY)
+
+    def by_comp(array):
+        return jnp.transpose(array, (1, 0, 2))
+
     rec_rows = ROW_REC * halves
     window = TILE_MOST * block_len
     incoming, messages = pl.pallas_call(
@@ -782,18 +817,33 @@
         ],
         compiler_params=pltpu.CompilerParams(collective_id=0, has_side_effects=True),
         name="render_step",
-    )(table, target, gaussians, across, first, second, power)
-
-    rates = np.ascontiguousarray(np.broadcast_to(learning_rates()[:, None], (comps, block_len)))
-    shape = jax.ShapeDtypeStruct(gaussians.shape, F32)
+    )(table, target, by_comp(gaussians), across, first, second, power)
+
+    rates = learning_rates() / BIAS_FIRST
+    shape = jax.ShapeDtypeStruct((comps, blocks, block_len), F32)
     new_params, new_one, new_two, mean_loss, gradient = pl.pallas_call(
         functools.partial(adam_kernel, geometry),
         out_shape=(shape, shape, shape, jax.ShapeDtypeStruct((1, 1), F32), shape),
-        in_specs=[vmem] * 6,
-        out_specs=(vmem,) * 5,
+        in_specs=[vmem, vmem, pl.BlockSpec(memory_space=pltpu.SMEM), vmem, hbm, hbm],
+        out_specs=(hbm, hbm, hbm, vmem, hbm),
+        scratch_shapes=[pltpu.VMEM((comps, blocks, block_len), F32)] * 4
+        + [pltpu.SemaphoreType.DMA((2,)), pltpu.SemaphoreType.DMA((4, PIECES))],
         name="adam_step",
-    )(messages, incoming, rates, gaussians, first_moment, second_moment)
-    return (new_params, new_one, new_two, mean_loss.reshape(()), gradient)
+    )(
+        messages,
+        incoming,
+        rates,
+        by_comp(gaussians),
+        by_comp(first_moment),
+        by_comp(second_moment),
+    )
+    return (
+        by_comp(new_params),
+        by_comp(new_one),
+        by_comp(new_two),
+        mean_loss.reshape(()),
+        by_comp(gradient),
+    )
 
 
 def solution(mesh):

time: 76.8 us -> 57.3 us (0.75)
  local copies, waits for them, and re-layouts: 16.8 us -> 3.3 us
  Pallas kernels: 58.9 us -> 52.9 us
    unnamed x25 -> x8, local copies, waits for them, and re-layouts: 16 us -> 2.52 us
    pallas_call x1, Pallas kernels: 51.8 us -> 47.1 us  [per_device(): pl.pallas_call(functools.partial(step_kernel, geometry), out_shape=(jax.S...]
    pallas_call x1, Pallas kernels: 7.12 us -> 5.83 us  [per_device(): pl.pallas_call(functools.partial(adam_kernel, geometry), out_shape=(shape...]
where the time goes in v2:
time: 57.3 us; the launch traced here: 57.1 us
  Pallas kernels  52.9 us (92%)
  local copies, waits for them, and re-layouts  3.3 us (6%)
  between operations  0.66 us (1%)
    pallas_call x1, Pallas kernels, per_device(): pl.pallas_call(functools.partial(step_kernel, geometry), out_shape=(jax.S...  47.1 us
    pallas_call x1, Pallas kernels, per_device(): pl.pallas_call(functools.partial(adam_kernel, geometry), out_shape=(shape...  5.83 us
    unnamed x8, local copies, waits for them, and re-layouts  2.52 us

profile of v2, /device:TPU:0, one launch (start us, length us, event | category | flops | bytes accessed | tf_op | source)
XLA Modules:
  0.0 57.1 jit_solution(4830119147338447355)
XLA Ops:
  0.6 0.0 copy-start.1
  0.6 0.6 %copy-done.1 = s32[1,1,16]{2,1,0:T(1,128)S(1)} copy-done((s32[1,1,16]{2,1,0:T(1,128)S(1)}, s32[1,1,16]{2,1,0:T(1,128)}, u32[]{:S(2)}) %copy-start.1) | copy-done | bytes 88
  1.3 0.0 copy-start.2
  1.3 0.7 %copy-done.2 = s32[1,1,8]{2,1,0:T(1,128)S(1)} copy-done((s32[1,1,8]{2,1,0:T(1,128)S(1)}, s32[1,1,8]{2,1,0:T(1,128)}, u32[]{:S(2)}) %copy-start.2) | copy-done | bytes 56
  1.9 0.0 copy-start.3
  2.0 0.1 add.26
  2.0 0.6 copy-done.3
  2.6 0.1 lt.18
  2.7 0.1 fusion
  2.8 0.0 copy-start
  2.8 0.6 %copy-done = f32[1,9]{1,0:T(1,128)S(1)} copy-done((f32[1,9]{1,0:T(1,128)S(1)}, f32[1,9]{1,0:T(1,128)}, u32[]{:S(2)}) %copy-start) | copy-done | bytes 60
  3.4 0.1 pad_maximum_fusion
  3.5 0.6 %broadcast_in_dim.14.table_ref = f32[17,1,128]{2,1,0:T(1,128)} reshape(f32[17,128]{1,0:T(8,128)S(1)} %pad_maximum_fusion) | data formatting | bytes 17408 | tf_op jit(solution)/shard_map/broadcast_in_dim | solution.py:779
  4.1 47.1 %render_step.1 = (f32[32,19,128]{2,1,0:T(8,128)}, f32[32,128]{1,0:T(8,128)}) custom-call(f32[17,1,128]{2,1,0:T(1,128)} %broadcast_in_dim.14.table_ref, f32[1,3,16,128]{3,2,1,0:T(8,128)} %target_ref.1, f32[62,16,256]{2,1,0:T(8,128)} %bitcast.12, f32[128,128]{1,0:T(8,128)} %constant.6.clone.across_ref, f32[96,120]{1,0:T(8,128)} %constant.16.clone.first_ref, ...), custom_call_target="tpu_custom_call" | custom-call | tf_op jit(solution)/shard_map/render_step/pallas_call | solution.py:791
  51.2 5.8 %adam_step.1 = (f32[62,16,256]{2,1,0:T(8,128)}, f32[62,16,256]{2,1,0:T(8,128)}, f32[62,16,256]{2,1,0:T(8,128)}, f32[1,1]{1,0:T(1,128)}, f32[62,16,256]{2,1,0:T(8,128)}) custom-call(f32[32,128]{1,0:T(8,128)} %get-tuple-element.12.messages_ref, f32[32,19,128]{2,1,0:T(8,128)} %get-tuple-element.13.incoming_ref, f32[62]{0:T(128)} %constant.19.clone.rates_ref, ...), custom_call_target="tpu_custom_call" | custom-call | tf_op jit(solution)/shard_map/adam_step/pallas_call | solution.py:824
  (6 shorter events, 0.0 us)
Async XLA Ops:
  0.6 0.7 %copy-start.1 = (s32[1,1,16]{2,1,0:T(1,128)S(1)}, s32[1,1,16]{2,1,0:T(1,128)}, u32[]{:S(2)}) copy-start(s32[1,1,16]{2,1,0:T(1,128)} %param.19) | copy-start | bytes 196
  1.3 0.7 %copy-start.2 = (s32[1,1,8]{2,1,0:T(1,128)S(1)}, s32[1,1,8]{2,1,0:T(1,128)}, u32[]{:S(2)}) copy-start(s32[1,1,8]{2,1,0:T(1,128)} %param.20) | copy-start | bytes 100
  1.9 0.7 %copy-start.3 = (s32[1,1,8]{2,1,0:T(1,128)S(1)}, s32[1,1,8]{2,1,0:T(1,128)}, u32[]{:S(2)}) copy-start(s32[1,1,8]{2,1,0:T(1,128)} %param.21) | copy-start | bytes 100
  2.8 0.7 %copy-start = (f32[1,9]{1,0:T(1,128)S(1)}, f32[1,9]{1,0:T(1,128)}, u32[]{:S(2)}) copy-start(f32[1,9]{1,0:T(1,128)} %param.17) | copy-start | bytes 112

commit v3 on v2

--- a/solution.py
+++ b/solution.py
@@ -14,6 +14,7 @@
 HALO = 5
 REACH = 2 * HALO
 ROW_REC = 9
+GEO_REC = 6
 PIECES = 4
 
 HIGHEST_MODE = lax.Precision.HIGHEST
@@ -224,18 +225,25 @@
 
 def step_kernel(
     geometry,
-    table_ref,
+    camera_ref,
+    list_ref,
+    start_ref,
+    end_ref,
     target_ref,
-    gauss_ref,
+    gauss_hbm,
     across_ref,
     first_ref,
     second_ref,
     power_ref,
     incoming_ref,
     messages_ref,
+    gauss_ref,
+    msg_out,
     msg_in,
-    rec_out,
-    rec_in,
+    geo_out,
+    geo_in,
+    tint_out,
+    tint_in,
     grad_out,
     grad_in,
     halo_out,
@@ -250,6 +258,7 @@
     recv_sem,
     halo_send,
     halo_recv,
+    fetch_sem,
 ):
     views_n, bands_n, blocks, list_len, rows, cols, block_len = geometry
     devices = views_n * bands_n
@@ -265,9 +274,15 @@
     has_down = band < bands_n - 1
 
     def peer_of(d):
-        peer = lax.rem(me + d, devices)
-        return (peer // bands_n, lax.rem(peer, bands_n))
-
+        return (lax.rem(view + d, views_n), lax.rem(band + d // views_n, bands_n))
+
+    fetch = pltpu.make_async_copy(gauss_hbm, gauss_ref, fetch_sem.at[0])
+    fetch.start()
+
+    msg_out[...] = jnp.zeros_like(msg_out)
+    msg_out[:, 0:9] = camera_ref[...]
+    list_row = list_ref[0].astype(F32)
+    msg_out[:, 16 : 16 + list_len] = list_row
     halo_in[...] = jnp.zeros_like(halo_in)
     thalo_in[...] = jnp.zeros_like(thalo_in)
     thalo_out[0] = target_ref[0, :, 0:REACH, :]
@@ -283,7 +298,8 @@
 
     def to_all(source_of, landing, phase):
         def send(d, carry):
-            peer = lax.rem(me + d, devices)
+            peer_view, peer_band = peer_of(d)
+            peer = peer_view * bands_n + peer_band
             pltpu.make_async_remote_copy(
                 src_ref=source_of(peer),
                 dst_ref=landing.at[me],
@@ -338,17 +354,22 @@
                 landing.at[1], landing.at[1], halo_recv.at[phase, 1]
             ).wait()
 
-    message = table_ref.at[0]
-    to_all(lambda peer: message, msg_in, 0)
+    to_all(lambda peer: msg_out, msg_in, 0)
     edges_start(thalo_out, thalo_in, 0)
-    msg_in[me] = table_ref[0]
-
-    list_row = table_ref[0][:, 16 : 16 + list_len]
+    msg_in[me] = msg_out[...]
+
     owner_low = lax.broadcasted_iota(jnp.int32, (devices, list_len), 0).astype(F32) * blocks
     owner_hot = jnp.where((list_row >= owner_low) & (list_row < owner_low + blocks), 1.0, 0.0)
-    place = jnp.concatenate(
-        [table_ref[1 + pair][:, 0:list_len] for pair in range(pairs)], axis=0
-    )
+    pair_row = lax.broadcasted_iota(jnp.int32, (pairs, tiles), 0)
+    on_tile = pair_row % tiles == lax.broadcasted_iota(jnp.int32, (pairs, tiles), 1)
+
+    def upright(row):
+        return jnp.sum(jnp.where(on_tile, row.astype(F32), 0.0), axis=1, keepdims=True)
+
+    later = (lax.broadcasted_iota(jnp.int32, (pairs, 1), 0) // tiles).astype(F32)
+    spot = upright(start_ref[0]) + later
+    position = lax.broadcasted_iota(jnp.int32, (pairs, list_len), 1).astype(F32)
+    place = jnp.where((position == spot) & (spot < upright(end_ref[0])), 1.0, 0.0)
     live_pair = jnp.max(place, axis=1, keepdims=True)
     pick_owner = lax.dot_general(
         place.astype(BF16), owner_hot.astype(BF16), (NT, ((), ())), preferred_element_type=F32
@@ -365,6 +386,7 @@
     )
 
     wait_all(msg_in, 0)
+    fetch.wait()
 
     asked = msg_in[...].reshape(devices, 128)
     messages_ref[...] = asked
@@ -386,24 +408,27 @@
         cam[0:6], [picked(6 + c) for c in range(3)], quats, picked(13)
     )
     records += [conic_a, conic_b, conic_c, opacity]
+    for p in range(GEO_REC):
+        for h in range(halves):
+            geo_out[:, p * halves + h, :] = records[p][:, h * 128 : (h + 1) * 128]
+    to_all(lambda peer: geo_out.at[peer], geo_in, 1)
+    geo_in[me] = geo_out[me]
     basis = camera_basis(cam)
     basis = [jnp.where(missing > 0.5, 0.0, value) for value in basis]
     for ch in range(3):
         colour = 0.5
         for q in range(16):
             colour = colour + basis[q] * picked(14 + 3 * q + ch)
-        records.append(colour)
-    for p in range(ROW_REC):
         for h in range(halves):
-            rec_out[:, p * halves + h, :] = records[p][:, h * 128 : (h + 1) * 128]
-    to_all(lambda peer: rec_out.at[peer], rec_in, 1)
-    rec_in[me] = rec_out[me]
-    wait_all(rec_in, 1)
-
-    def gathered(p):
+            tint_out[:, ch * halves + h, :] = colour[:, h * 128 : (h + 1) * 128]
+    to_all(lambda peer: tint_out.at[peer], tint_in, 2)
+    tint_in[me] = tint_out[me]
+    wait_all(geo_in, 1)
+
+    def gathered(landed, p):
         parts = []
         for h in range(halves):
-            parts.append(exact_dot(pick_owner, rec_in[:, p * halves + h, :], NN))
+            parts.append(exact_dot(pick_owner, landed[:, p * halves + h, :], NN))
         whole = jnp.concatenate(parts, axis=1)
         return jnp.concatenate(
             [whole[k * tiles : (k + 1) * tiles] for k in range(TILE_MOST)], axis=1
@@ -411,12 +436,12 @@
 
     dead = 1.0 - live
     tile_row = lax.broadcasted_iota(jnp.int32, (tiles, window), 0).astype(F32)
-    u_rel = gathered(0) - (tile_row * TILE + 0.5 * TILE)
-    w_rel = gathered(1) - ((band * rows).astype(F32) + 0.5 * TILE)
-    c_a = gathered(2) + dead
-    c_b = gathered(3)
-    c_c = gathered(4) + dead
-    opac = gathered(5) + dead
+    u_rel = gathered(geo_in, 0) - (tile_row * TILE + 0.5 * TILE)
+    w_rel = gathered(geo_in, 1) - ((band * rows).astype(F32) + 0.5 * TILE)
+    c_a = gathered(geo_in, 2) + dead
+    c_b = gathered(geo_in, 3)
+    c_c = gathered(geo_in, 4) + dead
+    opac = gathered(geo_in, 5) + dead
     inv_det = 1.0 / (c_a * c_c - c_b * c_b)
     coef_a = -0.5 * c_c * inv_det
     coef_b = c_b * inv_det
@@ -452,8 +477,9 @@
         power[0 : 2 * tiles],
     )
     coef[2] = expand_dot(masked(LOG2_E * coef_c), power[0:tiles])
+    wait_all(tint_in, 2)
     for ch in range(3):
-        coef[3 + ch] = expand_dot(masked(gathered(6 + ch)), power[0:tiles])
+        coef[3 + ch] = expand_dot(masked(gathered(tint_in, ch)), power[0:tiles])
 
     sub8 = lax.broadcasted_iota(jnp.int32, (8, cols), 0).astype(F32)
     parts_n = rows // 8
@@ -629,9 +655,9 @@
         for h in range(halves):
             grad_out[:, p * halves + h, :] = routed[:, h * 128 : (h + 1) * 128]
     grad_out[:, ROW_REC * halves, :] = jnp.broadcast_to(loss, (devices, 128))
-    to_all(lambda peer: grad_out.at[peer], grad_in, 2)
+    to_all(lambda peer: grad_out.at[peer], grad_in, 3)
     grad_in[me] = grad_out[me]
-    wait_all(grad_in, 2)
+    wait_all(grad_in, 3)
     incoming_ref[...] = grad_in[...]
 
 
@@ -760,23 +786,8 @@
     list_len = block_list.shape[2]
     rows, cols = target.shape[2:]
     tiles = cols // TILE
-    pairs = TILE_MOST * tiles
     halves = block_len // 128
     geometry = (views_n, bands_n, blocks, list_len, rows, cols, block_len)
-
-    message = jnp.concatenate(
-        [
-            camera,
-            jnp.zeros((1, 7), F32),
-            block_list[0].astype(F32),
-            jnp.zeros((1, 128 - 16 - list_len), F32),
-        ],
-        axis=1,
-    )
-    spot = tile_start[0, 0][None, :] + jnp.arange(TILE_MOST, dtype=jnp.int32)[:, None]
-    spot = jnp.where(spot < tile_end[0, 0][None, :], spot, -1).reshape(pairs, 1)
-    place = (spot == jnp.arange(128, dtype=jnp.int32)[None, :]).astype(F32)
-    table = jnp.concatenate([message, place], axis=0)[:, None, :]
 
     across, first, second = smoothing_tables(rows, cols, 3)
     power = power_table(tiles, cols)
@@ -794,12 +805,16 @@
             jax.ShapeDtypeStruct((devices, rec_rows + 1, 128), F32),
             jax.ShapeDtypeStruct((devices, 128), F32),
         ),
-        in_specs=[vmem] * 7,
+        in_specs=[vmem] * 5 + [hbm] + [vmem] * 4,
         out_specs=(vmem, vmem),
         scratch_shapes=[
+            pltpu.VMEM((comps, blocks, block_len), F32),
+            pltpu.VMEM((1, 128), F32),
             pltpu.VMEM((devices, 1, 128), F32),
-            pltpu.VMEM((devices, rec_rows, 128), F32),
-            pltpu.VMEM((devices, rec_rows, 128), F32),
+            pltpu.VMEM((devices, GEO_REC * halves, 128), F32),
+            pltpu.VMEM((devices, GEO_REC * halves, 128), F32),
+            pltpu.VMEM((devices, rec_rows - GEO_REC * halves, 128), F32),
+            pltpu.VMEM((devices, rec_rows - GEO_REC * halves, 128), F32),
             pltpu.VMEM((devices, rec_rows + 1, 128), F32),
             pltpu.VMEM((devices, rec_rows + 1, 128), F32),
             pltpu.VMEM((2, 3, REACH, cols), F32),
@@ -810,14 +825,26 @@
             pltpu.VMEM((window, rows // 8, 8, cols), F32),
             pltpu.VMEM((window, rows // 8, 8, cols), F32),
             pltpu.VMEM((6, window, cols), F32),
-            pltpu.SemaphoreType.DMA((3,)),
-            pltpu.SemaphoreType.DMA((3,)),
+            pltpu.SemaphoreType.DMA((4,)),
+            pltpu.SemaphoreType.DMA((4,)),
             pltpu.SemaphoreType.DMA((2, 2)),
             pltpu.SemaphoreType.DMA((2, 2)),
+            pltpu.SemaphoreType.DMA((1,)),
         ],
         compiler_params=pltpu.CompilerParams(collective_id=0, has_side_effects=True),
         name="render_step",
-    )(table, target, by_comp(gaussians), across, first, second, power)
+    )(
+        camera,
+        block_list,
+        tile_start,
+        tile_end,
+        target,
+        by_comp(gaussians),
+        across,
+        first,
+        second,
+        power,
+    )
 
     rates = learning_rates() / BIAS_FIRST
     shape = jax.ShapeDtypeStruct((comps, blocks, block_len), F32)

time: 57.3 us -> 50.6 us (0.88)
  local copies, waits for them, and re-layouts: 3.3 us -> 0 us
  Pallas kernels: 52.9 us -> 49.8 us
    pallas_call x1, Pallas kernels: 47.1 us -> 43.9 us  [per_device(): pl.pallas_call(functools.partial(step_kernel, geometry), out_shape=(jax.S...]
    unnamed x8 -> x0, local copies, waits for them, and re-layouts: 2.52 us -> none
    broadcast_in_dim x2 -> x0, local copies, waits for them, and re-layouts: 0.61 us -> none  [the longest x1 0.61 us: per_device(): table = jnp.concatenate([message, place], axis=0)[:, None, :]]
where the time goes in v3:
time: 50.6 us; the launch traced here: 50.4 us
  Pallas kernels  49.8 us (98%)
  between operations  0.64 us (1%)
    pallas_call x1, Pallas kernels, per_device(): pl.pallas_call(functools.partial(step_kernel, geometry), out_shape=(jax.S...  43.9 us
    pallas_call x1, Pallas kernels, per_device(): pl.pallas_call(functools.partial(adam_kernel, geometry), out_shape=(shape...  5.83 us

profile of v3, /device:TPU:0, one launch (start us, length us, event | category | flops | bytes accessed | tf_op | source)
XLA Modules:
  0.0 50.4 jit_solution(619486827050458678)
XLA Ops:
  0.6 43.9 %render_step.1 = (f32[32,19,128]{2,1,0:T(8,128)}, f32[32,128]{1,0:T(8,128)}) custom-call(f32[1,9]{1,0:T(1,128)} %camera_ref.1, s32[1,1,16]{2,1,0:T(1,128)} %list_ref.1, s32[1,1,8]{2,1,0:T(1,128)} %start_ref.1, s32[1,1,8]{2,1,0:T(1,128)} %end_ref.1, f32[1,3,16,128]{3,2,1,0:T(8,128)} %target_ref.1, f32[62,16,256]{2,1,0:T(8,128)} %bitcast.8, ...), custom_call_target="tpu_custom_call" | custom-call | tf_op jit(solution)/shard_map/render_step/pallas_call | solution.py:802
  44.6 5.8 %adam_step.1 = (f32[62,16,256]{2,1,0:T(8,128)}, f32[62,16,256]{2,1,0:T(8,128)}, f32[62,16,256]{2,1,0:T(8,128)}, f32[1,1]{1,0:T(1,128)}, f32[62,16,256]{2,1,0:T(8,128)}) custom-call(f32[32,128]{1,0:T(8,128)} %get-tuple-element.12.messages_ref, f32[32,19,128]{2,1,0:T(8,128)} %get-tuple-element.13.incoming_ref, f32[62]{0:T(128)} %constant.14.clone.rates_ref, ...), custom_call_target="tpu_custom_call" | custom-call | tf_op jit(solution)/shard_map/adam_step/pallas_call | solution.py:851
